TPU v7x, 256 devices: a whole 4x4x8 slice. The times are simulated.
256 devices in a mesh: gx: 4 (over x), gy: 4 (over z_hi), gz: 16 (over y, z_lo, core).
Axes of the slice: x: 4, y: 4, z: 8 (z_hi: 4, z_lo: 2; z = z_hi * 2 + z_lo), core: 2. Of those that a mesh axis runs over, the one named last changes fastest.
Arguments:
- position: float32 [3, 4, 4, 256, 128], P(None, 'gx', 'gy', 'gz'), may hold values from 0 to 1
- velocity: float32 [3, 4, 4, 256, 128], P(None, 'gx', 'gy', 'gz'), may hold values from -4 to 4
- radius: float32 [4, 4, 256, 128], P('gx', 'gy', 'gz'), may hold values from 0.06 to 0.1
- cell_count: int32 [4, 4, 256], P('gx', 'gy', 'gz'), may hold values from 16 to 128, as said below
- gas_velocity: float32 [3, 32, 32, 2048], P(None, 'gx', 'gy', 'gz'), may hold values from -3 to 3
- pressure: float32 [32, 32, 2048], P('gx', 'gy', 'gz'), may hold values from -5 to 5
Outputs:
- particle_position: float32 [3, 4, 4, 256, 128], P(None, 'gx', 'gy', 'gz')
- particle_velocity: float32 [3, 4, 4, 256, 128], P(None, 'gx', 'gy', 'gz')
- new_gas_velocity: float32 [3, 32, 32, 2048], P(None, 'gx', 'gy', 'gz')
- new_pressure: float32 [32, 32, 2048], P('gx', 'gy', 'gz')
Inputs may be any that keep to these rules, and one draw needn't show every extreme that they name: Slots 0 to cell_count - 1 of a DEM cell hold its particles, the others are empty.
All inputs are finite; a program needn't handle non-finite values.
Results may differ from a plain program's by a relative error of at most 0.0003.
Values sent between devices are 32-bit elements; how exact they have to be, the bound alone decides.
No kernel may reach another device: no remote copies, remote signals or barrier semaphores. Data moves between devices by JAX's collectives and lax.ppermute only.
A program may use at most 64 MiB of HBM per device.

v0:
```python
import math

import jax
import jax.numpy as jnp
from jax import lax
from jax.experimental import pallas as pl
from jax.experimental.pallas import tpu as pltpu
from jax.sharding import PartitionSpec as P

B = 8
S = 128
PZ = 16
SWEEPS = 3
DAMPING = 0.5
TIME_STEP = 0.005
GRAVITY = 1.0
SOFTENING = 0.0025
GAS_STEP = 0.2
GAS_DRAG = 2.0
PARTICLE_DRAG = 4.0
COUPLE_STEP = 0.25
LOWER_BOUND = 0.2
UPPER_BOUND = 2.0
UNIT_STEPS = ((1, 0, 0), (0, 1, 0), (0, 0, 1))

REACH = 0.194
FAR = 1e30
LZ = PZ + 2
NEAR = tuple((dx, dy, dz) for dx in (-1, 0, 1) for dy in (-1, 0, 1) for dz in (-1, 0, 1))
HIGHEST = lax.Precision.HIGHEST


def shift_pair(array_low, array_high, axis):
    count = lax.axis_size(axis)
    forward = [(i, i + 1) for i in range(count - 1)]
    backward = [(i + 1, i) for i in range(count - 1)]
    from_below = lax.ppermute(array_high, axis, forward)
    from_above = lax.ppermute(array_low, axis, backward)
    return from_below, from_above


def with_halo(block, sides, width):
    for axis, dim in sides:
        size = block.shape[dim]
        low, high = shift_pair(
            lax.slice_in_dim(block, 0, width, axis=dim),
            lax.slice_in_dim(block, size - width, size, axis=dim),
            axis,
        )
        block = jnp.concatenate([low, block, high], axis=dim)
    return block


def chebyshev_factor(sweep_index, sweeps):
    centre = 0.5 * (UPPER_BOUND + LOWER_BOUND)
    radius_half = 0.5 * (UPPER_BOUND - LOWER_BOUND)
    return 1.0 / (centre + radius_half * math.cos(math.pi * (2 * sweep_index + 1) / (2 * sweeps)))


def lane_iota(rows):
    return lax.broadcasted_iota(jnp.int32, (rows, S), 1)


def axis_weights(row):
    centres = lax.broadcasted_iota(jnp.int32, (B, S), 0).astype(jnp.float32) + 0.5
    gap = jnp.broadcast_to(row, (B, S)) * float(B) - centres
    kernel = jnp.exp(-gap * gap)
    return kernel / jnp.sum(kernel, axis=0, keepdims=True)


def plane_weights(row_x, row_y):
    wx = axis_weights(row_x)
    wy = axis_weights(row_y)
    return jnp.concatenate(
        [jnp.broadcast_to(wx[a : a + 1], (B, S)) * wy for a in range(B)], axis=0
    )


def contact_kernel(deposit, *refs):
    p_own, p_ylo, p_yhi, p_xlo, p_xhi, r_own, r_ylo, r_yhi, r_xlo, r_xhi = refs[:10]
    out_ref = refs[10]
    rest = refs[11:]
    if deposit:
        dep_ref = rest[0]
        rest = rest[1:]
    mask_s, pref_s, work_s, key_s, list_s, own_s, force_s, rows_s, slots_s = rest[:9]

    def source(dx, dy):
        if dx == 0:
            return ((p_ylo, p_own, p_yhi)[dy + 1], 0, (r_ylo, r_own, r_yhi)[dy + 1], 6 * LZ)
        p_ref, r_ref = (p_xlo, r_xlo) if dx < 0 else (p_xhi, r_xhi)
        return (
            p_ref,
            (dy + 1) * (p_ref.shape[0] // 3),
            r_ref,
            (dy + 1) * (r_ref.shape[0] // 3) + 6 * LZ,
        )

    lane = lane_iota(8)
    tri_row = lax.broadcasted_iota(jnp.int32, (S, 2 * S), 0)
    tri_col = lax.broadcasted_iota(jnp.int32, (S, 2 * S), 1)
    tri = jnp.where((tri_row < tri_col) | (tri_col >= S), 1.0, 0.0).astype(jnp.bfloat16)

    for half in range(2):
        first = 1 + 8 * half
        own_r = r_own[6 * LZ + first : 6 * LZ + first + 8, :]
        own_live = own_r > 0.0
        bounds = []
        for f in range(3):
            value = p_own[f * LZ + first : f * LZ + first + 8, :]
            top = jnp.max(jnp.where(own_live, value, -FAR), axis=1, keepdims=True) + REACH
            bottom = jnp.min(jnp.where(own_live, value, FAR), axis=1, keepdims=True) - REACH
            bounds.append((jnp.broadcast_to(bottom, (8, S)), jnp.broadcast_to(top, (8, S))))
        used = jnp.max(
            jnp.where(own_live, (lane + 1).astype(jnp.float32), 0.0), axis=1, keepdims=True
        )
        for k, offset in enumerate(NEAR):
            p_ref, p_base, r_ref, r_base = source(offset[0], offset[1])
            row = first + offset[2]
            keep = r_ref[r_base + row : r_base + row + 8, :] > 0.0
            for f in range(3):
                start = p_base + f * LZ + row
                value = p_ref[start : start + 8, :] + float(offset[f])
                keep = keep & (value >= bounds[f][0]) & (value <= bounds[f][1])
            mask_s[k * 8 : k * 8 + 8, :] = jnp.where(keep, 1.0, 0.0)
        pref_s[...] = jnp.dot(
            mask_s[...].astype(jnp.bfloat16), tri, preferred_element_type=jnp.float32
        )
        base = jnp.zeros((8, S), jnp.int32)
        for k, offset in enumerate(NEAR):
            before = pref_s[k * 8 : k * 8 + 8, 0:S].astype(jnp.int32)
            count = pref_s[k * 8 : k * 8 + 8, S : 2 * S].astype(jnp.int32)
            hop = jnp.where(mask_s[k * 8 : k * 8 + 8, :] > 0.0, lane - before, 0)
            for bit in range(7):
                step = 1 << bit
                moved = pltpu.roll(hop, S - step, 1)
                hop = jnp.where(
                    (moved & step) != 0, moved, jnp.where((hop & step) != 0, 0, hop)
                )
            slot = (lane - base) & (S - 1)
            pick = (jnp.take_along_axis(hop, slot, axis=1) + slot) & (S - 1)
            page = (base >> 7) + jnp.where(lane < (base & (S - 1)), 1, 0)
            key_s[k * 8 : k * 8 + 8, :] = jnp.where(slot < count, page, -1)
            base = base + count
            p_ref, p_base, r_ref, r_base = source(offset[0], offset[1])
            row = first + offset[2]
            for f in range(7):
                if f < 6:
                    start = p_base + f * LZ + row
                    value = p_ref[start : start + 8, :]
                    if f < 3 and offset[f] != 0:
                        value = value + float(offset[f])
                else:
                    value = r_ref[r_base + row : r_base + row + 8, :]
                work_s[k, f] = jnp.take_along_axis(value, pick, axis=1)
        total = base.astype(jnp.float32)
        pages = (jnp.max(total).astype(jnp.int32) + (S - 1)) >> 7
        for i in range(8):
            rows_s[half * 8 + i] = (
                jnp.max(total[i : i + 1, :]).astype(jnp.int32) + (S - 1)
            ) >> 7
            slots_s[half * 8 + i] = jnp.max(used[i : i + 1, :]).astype(jnp.int32)

        def merge(page, carry):
            acc = [jnp.zeros((8, S), jnp.float32)] * 6 + [jnp.full((8, S), -10.0, jnp.float32)]
            for k in range(27):
                here = key_s[k * 8 : k * 8 + 8, :] == page
                acc = [jnp.where(here, work_s[k, f], acc[f]) for f in range(7)]
            for f in range(7):
                list_s[page, f, half * 8 : half * 8 + 8, :] = acc[f]
            return carry

        lax.fori_loop(0, pages, merge, 0)

    live = r_own[6 * LZ + 1 : 6 * LZ + 17, :] > 0.0
    radius = r_own[6 * LZ + 1 : 6 * LZ + 17, :]
    own_rows = [p_own[f * LZ + 1 : f * LZ + 17, :] for f in range(6)]
    own_rows.append(jnp.where(live, radius, -10.0))
    own_rows.append(jnp.zeros((16, S), jnp.float32))
    own_s[...] = jnp.concatenate(own_rows, axis=0).T
    force_s[...] = jnp.zeros((S, S), jnp.float32)

    def one_cell(cell, carry):
        page_count = rows_s[cell]
        slot_count = slots_s[cell]
        for group in range(4):

            @pl.when(slot_count > 32 * group)
            def _():
                own = []
                for t in range(4):
                    tile = own_s[32 * group + 8 * t : 32 * group + 8 * t + 8, :]
                    own.append(
                        [
                            jnp.take_along_axis(
                                tile, jnp.full((8, S), f * 16, jnp.int32) + cell, axis=1
                            )
                            for f in range(7)
                        ]
                    )

                def near_page(page, acc):
                    near = [
                        jnp.broadcast_to(list_s[page, f, pl.ds(cell, 1), :], (8, S))
                        for f in range(7)
                    ]
                    out = []
                    for t in range(4):
                        ex = near[0] - own[t][0]
                        ey = near[1] - own[t][1]
                        ez = near[2] - own[t][2]
                        square = ex * ex + ey * ey + ez * ez + SOFTENING
                        inverse = lax.rsqrt(square)
                        press = jnp.maximum((near[6] + own[t][6]) - square * inverse, 0.0)
                        closing = (
                            (near[3] - own[t][3]) * ex
                            + (near[4] - own[t][4]) * ey
                            + (near[5] - own[t][5]) * ez
                        )
                        size = press * inverse * (1.0 - DAMPING * (closing * inverse))
                        out.append(acc[3 * t] + size * ex)
                        out.append(acc[3 * t + 1] + size * ey)
                        out.append(acc[3 * t + 2] + size * ez)
                    return tuple(out)

                zero = jnp.zeros((8, S), jnp.float32)
                acc = lax.fori_loop(0, page_count, near_page, (zero,) * 12)
                for t in range(4):
                    rows = slice(32 * group + 8 * t, 32 * group + 8 * t + 8)
                    tile = force_s[rows, :]
                    for f in range(3):
                        total_f = jnp.sum(acc[3 * t + f], axis=1, keepdims=True)
                        tile = jnp.where(
                            lane == f * 16 + cell, jnp.broadcast_to(total_f, (8, S)), tile
                        )
                    force_s[rows, :] = tile

        return carry

    lax.fori_loop(0, PZ, one_cell, 0)

    force = force_s[...].T
    scale = jnp.where(live, -1.0 / (radius * radius * radius), 0.0)
    for f in range(3):
        push = force[f * 16 : f * 16 + 16, :] * scale
        if f == 2:
            push = push - GRAVITY
        speed = p_own[(3 + f) * LZ + 1 : (3 + f) * LZ + 17, :] + TIME_STEP * push
        place = p_own[f * LZ + 1 : f * LZ + 17, :] + TIME_STEP * speed
        out_ref[f * 16 : f * 16 + 16, :] = place
        out_ref[(3 + f) * 16 : (3 + f) * 16 + 16, :] = speed

    if deposit:
        dep_s = rest[9]

        def one_deposit(cell, carry):
            def row(f):
                return out_ref[pl.ds(f * 16 + cell, 1), :]

            r = r_own[pl.ds(6 * LZ + 1 + cell, 1), :]
            volume = (4.0 * math.pi / 3.0 * B**3) * (r * r * r)
            plane = plane_weights(row(0), row(1))
            wz = axis_weights(row(2))
            carried = [volume, volume * row(3), volume * row(4), volume * row(5)]
            left = jnp.concatenate(
                [jnp.broadcast_to(c, (B, S)) * wz for c in carried], axis=0
            )
            block = lax.dot_general(
                left,
                plane,
                (((1,), (1,)), ((), ())),
                precision=HIGHEST,
                preferred_element_type=jnp.float32,
            )
            for f in range(4):
                dep_s[f, pl.ds(pl.multiple_of(cell * 8, 8), 8), 0:64] = block[
                    f * 8 : f * 8 + 8, :
                ]
            return carry

        lax.fori_loop(0, PZ, one_deposit, 0)
        for f in range(4):
            dep_ref[f * 64 : f * 64 + 64, :] = dep_s[f].T[0:64, :]


def contact(deposit, places, radii):
    shapes = [jax.ShapeDtypeStruct((96, S), jnp.float32)]
    scratch = [
        pltpu.VMEM((27 * 8, S), jnp.float32),
        pltpu.VMEM((27 * 8, 2 * S), jnp.float32),
        pltpu.VMEM((27, 7, 8, S), jnp.float32),
        pltpu.VMEM((27 * 8, S), jnp.int32),
        pltpu.VMEM((27, 7, 16, S), jnp.float32),
        pltpu.VMEM((S, S), jnp.float32),
        pltpu.VMEM((S, S), jnp.float32),
        pltpu.SMEM((16,), jnp.int32),
        pltpu.SMEM((16,), jnp.int32),
    ]
    if deposit:
        shapes.append(jax.ShapeDtypeStruct((256, S), jnp.float32))
        scratch.append(pltpu.VMEM((4, S, S), jnp.float32))
    return pl.pallas_call(
        lambda *refs: contact_kernel(deposit, *refs),
        out_shape=shapes,
        scratch_shapes=scratch,
        name="contact_deposit" if deposit else "contact",
    )(*places, *radii)


def sample_kernel(field_ref, state_ref, out_ref, field_s, pair_s, sum_s):
    for v in range(3):
        field_s[:, v * S : v * S + S] = field_ref[v * S : v * S + S, :].T
    pair_s[...] = jnp.zeros((S, 2 * S), jnp.float32)

    def one_cell(cell, carry):
        def row(f):
            return state_ref[pl.ds(f * 16 + cell, 1), :]

        plane = plane_weights(row(0), row(1))
        wz = axis_weights(row(2))
        pair_s[0:64, 0:S] = plane
        pair_s[64:S, S : 2 * S] = plane
        start = pl.multiple_of(cell * 8, 8)
        left = jnp.concatenate(
            [field_s[pl.ds(start, 8), v * S : v * S + S] for v in range(3)], axis=0
        )
        part = jnp.dot(
            left, pair_s[...], precision=HIGHEST, preferred_element_type=jnp.float32
        )
        for v in range(3):
            for odd in range(2):
                value = part[v * 8 : v * 8 + 8, odd * S : odd * S + S] * wz
                sum_s[pl.ds((2 * v + odd) * 16 + cell, 1), :] = jnp.sum(
                    value, axis=0, keepdims=True
                )
        return carry

    lax.fori_loop(0, PZ, one_cell, 0)
    for f in range(3):
        speed = state_ref[(3 + f) * 16 : (3 + f) * 16 + 16, :]
        gas = sum_s[f * 16 : f * 16 + 16, :]
        slope = sum_s[(3 + f) * 16 : (3 + f) * 16 + 16, :]
        out_ref[f * 16 : f * 16 + 16, :] = (
            speed + COUPLE_STEP * (PARTICLE_DRAG * gas - slope)
        ) / (1.0 + COUPLE_STEP * PARTICLE_DRAG)


def sample(fields, state):
    return pl.pallas_call(
        sample_kernel,
        out_shape=jax.ShapeDtypeStruct((48, S), jnp.float32),
        scratch_shapes=[
            pltpu.VMEM((S, 3 * S), jnp.float32),
            pltpu.VMEM((S, 2 * S), jnp.float32),
            pltpu.VMEM((96, S), jnp.float32),
        ],
        name="sample",
    )(fields, state)


def inner(padded, offset=(0, 0, 0)):
    sizes = padded.shape[-3:]
    return padded[
        ...,
        1 + offset[0] : sizes[0] - 1 + offset[0],
        1 + offset[1] : sizes[1] - 1 + offset[1],
        1 + offset[2] : sizes[2] - 1 + offset[2],
    ]


def centred(padded, direction):
    forward = UNIT_STEPS[direction]
    backward = tuple(-c for c in forward)
    return (inner(padded, forward) - inner(padded, backward)) * 0.5


def neighbours(padded):
    return sum(
        inner(padded, tuple(sign * c for c in step)) for step in UNIT_STEPS for sign in (1, -1)
    )


def inside(width):
    keep = None
    for dim, (axis, size) in enumerate((("gx", B), ("gy", B), ("gz", S))):
        index = lax.broadcasted_iota(
            jnp.int32, (B + 2 * width, B + 2 * width, S + 2 * width), dim
        )
        place = lax.axis_index(axis) * size + index - width
        good = (place >= 0) & (place < lax.axis_size(axis) * size)
        keep = good if keep is None else keep & good
    return keep


def gas_inputs(gas_velocity, pressure):
    wide = with_halo(
        jnp.concatenate([gas_velocity, pressure[None]], axis=0),
        (("gy", 2), ("gx", 1), ("gz", 3)),
        5,
    )
    velocity = wide[:3]
    middle = inner(velocity)
    transport = sum(middle[d] * centred(velocity, d) for d in range(3))
    return middle - GAS_STEP * transport, inner(wide[3])


def gas_step(deposits, pulled, pressure):
    wide = with_halo(deposits, (("gy", 2), ("gx", 1), ("gz", 3)), 4)
    solids = wide[0]
    voidage = 1.0 / (1.0 + solids)
    intermediate = (voidage * pulled + GAS_STEP * GAS_DRAG * wide[1:4]) / (
        voidage + GAS_STEP * GAS_DRAG * solids
    )
    flux = voidage * intermediate
    source = -sum(centred(flux[d], d) for d in range(3)) / GAS_STEP
    diagonal = inner(6.0 + voidage)
    current = pressure
    for sweep in range(SWEEPS):
        if sweep > 0:
            source = inner(source)
            diagonal = inner(diagonal)
        factor = chebyshev_factor(sweep, SWEEPS)
        middle = inner(current)
        updated = middle + factor * (
            source - diagonal * middle + neighbours(current)
        ) / diagonal
        current = jnp.where(inside(3 - sweep), updated, 0.0)
    gradient = jnp.stack([centred(current, d) for d in range(3)])
    return intermediate[:, 4:-4, 4:-4, 4:-4] - GAS_STEP * gradient, inner(current), gradient


def body(position, velocity, radius, cell_count, gas_velocity, pressure):
    rank = lax.axis_index("gz")
    ranks = lax.axis_size("gz")
    live = jnp.arange(S, dtype=jnp.int32) < cell_count[0, 0][:, None]
    kept = jnp.where(live, radius[0, 0], 0.0)
    state = jnp.concatenate([position[:, 0, 0], velocity[:, 0, 0], kept[None]], axis=0)
    rows = jnp.swapaxes(state, 0, 1)
    blank = jnp.zeros_like(rows[:1])
    below = jnp.concatenate([blank, rows[:-1]], axis=0)
    above = jnp.concatenate([rows[1:], blank], axis=0)
    extra = jnp.where(rank == ranks - 1, below, jnp.where(rank == 0, above, 0.0))
    sent = jnp.stack([rows, extra], axis=1).reshape(PZ, 14 * S)
    got = lax.all_to_all(sent, "gz", split_axis=0, concat_axis=0, tiled=True)
    got = got.reshape(PZ, 2, 7, S)
    layers = jnp.concatenate([got[PZ - 1 :, 1], got[:, 0], got[:1, 1]], axis=0)
    own = jnp.swapaxes(layers, 0, 1).reshape(7 * LZ, S)

    pulled, wide_pressure = gas_inputs(gas_velocity, pressure)

    def around(block):
        ylo, yhi = shift_pair(block, block, "gy")
        column = jnp.concatenate([ylo, block, yhi], axis=0)
        xlo, xhi = shift_pair(column, column, "gx")
        return (block, ylo, yhi, xlo, xhi)

    first = around(own)
    (moved,) = contact(False, first, first)
    moved = moved.reshape(6, PZ, S)
    zlo, zhi = shift_pair(moved[:, :1], moved[:, PZ - 1 :], "gz")
    middle = jnp.concatenate([zlo, moved, zhi], axis=1).reshape(6 * LZ, S)
    second = around(middle)
    final, deposits = contact(True, second, first)

    new_velocity, new_pressure, gradient = gas_step(
        deposits.reshape(4, B, B, S), pulled, wide_pressure
    )
    fields = jnp.concatenate([new_velocity, gradient], axis=0).reshape(6 * B * B, S)
    speed = sample(fields, final)

    def back(array):
        count = array.shape[0] // PZ
        sent_back = jnp.swapaxes(array.reshape(count, PZ, S), 0, 1).reshape(PZ, count * S)
        returned = lax.all_to_all(sent_back, "gz", split_axis=0, concat_axis=0, tiled=True)
        return jnp.swapaxes(returned.reshape(PZ, count, S), 0, 1)[:, None, None]

    return (back(final[:48]), back(speed), new_velocity, new_pressure)


def solution(mesh):
    placed = (
        P(None, "gx", "gy", "gz", None),
        P(None, "gx", "gy", "gz", None),
        P("gx", "gy", "gz", None),
        P("gx", "gy", "gz"),
        P(None, "gx", "gy", "gz"),
        P("gx", "gy", "gz"),
    )
    return jax.shard_map(
        body,
        mesh=mesh,
        in_specs=placed,
        out_specs=(
            P(None, "gx", "gy", "gz", None),
            P(None, "gx", "gy", "gz", None),
            P(None, "gx", "gy", "gz"),
            P("gx", "gy", "gz"),
        ),
        check_vma=False,
    )
```

profile of v0, /device:TPU:1, one launch (start us, length us, event | category | flops | bytes accessed | tf_op | source)
XLA Modules:
  0.0 198.8 jit_solution(5709447603710110269)
XLA Ops:
  3.1 7.3 %all-to-all-start = ((f32[16,1,1792]{2,1,0:T(1,128)}), f32[16,1,1792]{2,1,0:T(1,128)S(1)}, u32[]{:S(2)}, u32[]{:S(2)}) async-start(f32[16,1,1792]{2,1,0:T(1,128)} %all_to_all.24), calls=%async_computation | async-start | bytes 229376 | tf_op jit(solution)/shard_map/all_to_all | solution.py:444
  11.4 4.9 %collective-permute-start.16 = (f32[4,8,5,128]{3,2,1,0:T(8,128)S(1)}, f32[4,8,5,128]{3,2,1,0:T(8,128)S(1)}, u32[]{:S(2)}, u32[]{:S(2)}) collective-permute-start(f32[4,8,5,128]{3,2,1,0:T(8,128)S(1)} %get-tuple-element.48), channel_id=1, source_target_pairs={{0,16},{16,32},{32,48},{1,17},{17,33},{33,49},{2,18},{18,34},{34,5... | collective-permute-start | bytes 245768 | tf_op jit(solution)/shard_map/ppermute | solution.py:37
  20.3 5.8 %collective-permute-start = (f32[126,128]{1,0:T(8,128)S(1)}, f32[126,128]{1,0:T(8,128)S(1)}, u32[]{:S(2)}, u32[]{:S(2)}) collective-permute-start(f32[126,128]{1,0:T(8,128)S(1)} %reshape.115.refs_0_.refs_5_), channel_id=1, source_target_pairs={{0,16},{16,32},{32,48},{1,17},{17,33},{33,49},{2,18},{18,34},{34,5... | collective-permute-start | bytes 193544 | tf_op jit(solution)/shard_map/ppermute | solution.py:37
  27.6 5.7 %collective-permute-done.1.refs_2_.refs_7_ = f32[126,128]{1,0:T(8,128)S(1)} collective-permute-done((f32[126,128]{1,0:T(8,128)S(1)}, f32[126,128]{1,0:T(8,128)S(1)}, u32[]{:S(2)}, u32[]{:S(2)}) %collective-permute-start.1) | collective-permute-done | bytes 64544 | tf_op jit(solution)/shard_map/ppermute | solution.py:38
  33.3 3.1 %collective-permute-start.2 = (f32[378,128]{1,0:T(8,128)S(1)}, f32[378,128]{1,0:T(8,128)S(1)}, u32[]{:S(2)}, u32[]{:S(2)}) collective-permute-start(f32[378,128]{1,0:T(8,128)S(1)} %pad_maximum_fusion.12), channel_id=1, source_target_pairs={{0,64},{64,128},{128,192},{1,65},{65,129},{129,193},{2,66},{66,130... | collective-permute-start | bytes 580616 | tf_op jit(solution)/shard_map/ppermute | solution.py:37
  37.8 4.0 %collective-permute-start.18 = (f32[4,5,18,128]{3,2,1,0:T(8,128)S(1)}, f32[4,5,18,128]{3,2,1,0:T(8,128)S(1)}, u32[]{:S(2)}, u32[]{:S(2)}) collective-permute-start(f32[4,5,18,128]{3,2,1,0:T(8,128)S(1)} %get-tuple-element.36), channel_id=1, source_target_pairs={{0,64},{64,128},{128,192},{1,65},{65,129},{129,193},{2,66},{66,130... | collective-permute-start | bytes 552968 | tf_op jit(solution)/shard_map/ppermute | solution.py:37
  41.8 1.3 collective-permute-start.19
  44.4 22.0 %contact.1 = f32[96,128]{1,0:T(8,128)} custom-call(f32[126,128]{1,0:T(8,128)} %copy-done.4, f32[126,128]{1,0:T(8,128)} %copy-done.14, f32[126,128]{1,0:T(8,128)} %copy-done.15, f32[378,128]{1,0:T(8,128)} %copy-done.2, f32[378,128]{1,0:T(8,128)} %copy-done.3, f32[126,128]{1,0:T(8,128)} %copy-done.4, f32[126,128]{1,0:T(8,128)} %copy-done.14, ...), custom_call_target="tpu_custom_call" | custom-call | tf_op jit(solution)/shard_map/contact/pallas_call | solution.py:302
  67.2 6.7 %collective-permute-start.4 = (f32[6,1,128]{2,1,0:T(1,128)S(1)}, f32[6,1,128]{2,1,0:T(1,128)S(1)}, u32[]{:S(2)}, u32[]{:S(2)}) collective-permute-start(f32[6,1,128]{2,1,0:T(1,128)S(1)} %get-tuple-element.56), channel_id=1, source_target_pairs={{0,1},{1,2},{2,3},{3,4},{4,5},{5,6},{6,7},{7,8},{8,9},{9,10},{10,1... | collective-permute-start | bytes 9224 | tf_op jit(solution)/shard_map/ppermute | solution.py:37
  73.9 1.9 collective-permute-start.5
  76.3 2.5 %collective-permute-done.5 = f32[6,1,128]{2,1,0:T(1,128)S(1)} collective-permute-done((f32[6,1,128]{2,1,0:T(1,128)S(1)}, f32[6,1,128]{2,1,0:T(1,128)S(1)}, u32[]{:S(2)}, u32[]{:S(2)}) %collective-permute-start.5) | collective-permute-done | bytes 3104 | tf_op jit(solution)/shard_map/ppermute | solution.py:38
  79.7 6.6 %collective-permute-start.6 = (f32[108,128]{1,0:T(8,128)S(1)}, f32[108,128]{1,0:T(8,128)S(1)}, u32[]{:S(2)}, u32[]{:S(2)}) collective-permute-start(f32[108,128]{1,0:T(8,128)S(1)} %reshape.117.refs_0_), channel_id=1, source_target_pairs={{0,16},{16,32},{32,48},{1,17},{17,33},{33,49},{2,18},{18,34},{34,5... | collective-permute-start | bytes 165896 | tf_op jit(solution)/shard_map/ppermute | solution.py:37
  87.8 4.3 %collective-permute-done.7.refs_2_ = f32[108,128]{1,0:T(8,128)S(1)} collective-permute-done((f32[108,128]{1,0:T(8,128)S(1)}, f32[108,128]{1,0:T(8,128)S(1)}, u32[]{:S(2)}, u32[]{:S(2)}) %collective-permute-start.7) | collective-permute-done | bytes 55328 | tf_op jit(solution)/shard_map/ppermute | solution.py:38
  92.8 5.9 %collective-permute-start.8 = (f32[324,128]{1,0:T(8,128)}, f32[324,128]{1,0:T(8,128)}, u32[]{:S(2)}, u32[]{:S(2)}) collective-permute-start(f32[324,128]{1,0:T(8,128)} %pad_maximum_fusion.14), channel_id=1, source_target_pairs={{0,64},{64,128},{128,192},{1,65},{65,129},{129,193},{2,66},{66,130... | collective-permute-start | bytes 497672 | tf_op jit(solution)/shard_map/ppermute | solution.py:37
  100.9 3.0 %collective-permute-start.20 = (f32[4,18,18,5]{2,0,3,1:T(4,128)S(1)}, f32[4,18,18,5]{2,0,3,1:T(4,128)S(1)}, u32[]{:S(2)}, u32[]{:S(2)}) collective-permute-start(f32[4,18,18,5]{2,0,3,1:T(4,128)S(1)} %copy.45), channel_id=1, source_target_pairs={{0,1},{1,2},{2,3},{3,4},{4,5},{5,6},{6,7},{7,8},{8,9},{9,10},{10,1... | collective-permute-start | bytes 77768 | tf_op jit(solution)/shard_map/ppermute | solution.py:37
  104.5 1.9 collective-permute-start.21
  107.5 3.9 %collective-permute-done.21 = f32[4,18,18,5]{2,0,3,1:T(4,128)S(1)} collective-permute-done((f32[4,18,18,5]{2,0,3,1:T(4,128)S(1)}, f32[4,18,18,5]{2,0,3,1:T(4,128)S(1)}, u32[]{:S(2)}, u32[]{:S(2)}) %collective-permute-start.21) | collective-permute-done | bytes 25952 | tf_op jit(solution)/shard_map/ppermute | solution.py:38
  112.0 25.3 %contact_deposit.1 = (f32[96,128]{1,0:T(8,128)}, f32[256,128]{1,0:T(8,128)}) custom-call(f32[108,128]{1,0:T(8,128)} %copy-done.22, f32[108,128]{1,0:T(8,128)} %copy-done.24, f32[108,128]{1,0:T(8,128)} %copy-done.25, f32[324,128]{1,0:T(8,128)} %collective-permute-done.8.refs_3_, f32[324,128]{1,0:T(8,128)} %collective-permute-done.9.refs_4_, ...), custom_call_target="tpu_custom_call" | custom-call | tf_op jit(solution)/shard_map/contact_deposit/pallas_call | solution.py:302
  138.2 3.5 %collective-permute-start.10 = (f32[4,8,4,128]{3,2,1,0:T(4,128)S(1)}, f32[4,8,4,128]{3,2,1,0:T(4,128)S(1)}, u32[]{:S(2)}, u32[]{:S(2)}) collective-permute-start(f32[4,8,4,128]{3,2,1,0:T(4,128)S(1)} %get-tuple-element.46), channel_id=1, source_target_pairs={{0,16},{16,32},{32,48},{1,17},{17,33},{33,49},{2,18},{18,34},{34,5... | collective-permute-start | bytes 196616 | tf_op jit(solution)/shard_map/ppermute | solution.py:37
  141.7 1.4 collective-permute-start.11
  143.1 2.2 %pad_maximum_fusion = f32[4,18,18,138]{3,2,1,0:T(8,128)S(1)} fusion(f32[4,18,18,5]{3,2,1,0:T(8,128)S(1)} %copy.48, f32[4,5,18,128]{3,2,1,0:T(8,128)} %copy-done.20, f32[4,8,5,128]{3,2,1,0:T(8,128)} %copy-done.9, f32[1,8,8,128]{3,2,1,0:T(8,128)} %bitcast.71, f32[3,8,8,128]{3,2,1,0:T(8,128)} %param.10, f32[4,8,5,128]{3,2,1,0:T(8,128)} %copy-done.8, ...), kind=kLoop, calls=%fused_computation | loop fusion | flops 1251936 | bytes 1430784 | tf_op jit(solution)/shard_map/concatenate | solution.py:50
  145.3 2.4 %collective-permute-done.11 = f32[4,8,4,128]{3,2,1,0:T(4,128)S(1)} collective-permute-done((f32[4,8,4,128]{3,2,1,0:T(4,128)S(1)}, f32[4,8,4,128]{3,2,1,0:T(4,128)S(1)}, u32[]{:S(2)}, u32[]{:S(2)}) %collective-permute-start.11) | collective-permute-done | bytes 65568 | tf_op jit(solution)/shard_map/ppermute | solution.py:38
  147.8 6.6 %collective-permute-start.12 = (f32[4,4,16,128]{3,2,1,0:T(8,128)S(1)}, f32[4,4,16,128]{3,2,1,0:T(8,128)S(1)}, u32[]{:S(2)}, u32[]{:S(2)}) collective-permute-start(f32[4,4,16,128]{3,2,1,0:T(8,128)S(1)} %get-tuple-element.40), channel_id=1, source_target_pairs={{0,64},{64,128},{128,192},{1,65},{65,129},{129,193},{2,66},{66,130... | collective-permute-start | bytes 393224 | tf_op jit(solution)/shard_map/ppermute | solution.py:37
  156.8 3.3 %collective-permute-done.13 = f32[4,4,16,128]{3,2,1,0:T(8,128)S(1)} collective-permute-done((f32[4,4,16,128]{3,2,1,0:T(8,128)S(1)}, f32[4,4,16,128]{3,2,1,0:T(8,128)S(1)}, u32[]{:S(2)}, u32[]{:S(2)}) %collective-permute-start.13) | collective-permute-done | bytes 131104 | tf_op jit(solution)/shard_map/ppermute | solution.py:38
  161.4 3.6 %collective-permute-start.14 = (f32[4,16,16,4]{3,2,1,0:T(8,128)}, f32[4,16,16,4]{3,2,1,0:T(8,128)S(1)}, u32[]{:S(2)}, u32[]{:S(2)}) collective-permute-start(f32[4,16,16,4]{3,2,1,0:T(8,128)} %get-tuple-element.34), channel_id=1, source_target_pairs={{0,1},{1,2},{2,3},{3,4},{4,5},{5,6},{6,7},{7,8},{8,9},{9,10},{10,1... | collective-permute-start | bytes 49160 | tf_op jit(solution)/shard_map/ppermute | solution.py:37
  165.0 1.9 collective-permute-start.15
  167.6 3.6 %all-to-all-start.1 = ((f32[16,1,384]{2,1,0:T(1,128)}), f32[16,1,384]{2,1,0:T(1,128)S(1)}, u32[]{:S(2)}, u32[]{:S(2)}) async-start(f32[16,1,384]{2,1,0:T(1,128)} %all_to_all.25), calls=%async_computation.1 | async-start | bytes 49152 | tf_op jit(solution)/shard_map/all_to_all | solution.py:474
  171.4 6.1 %collective-permute-done.15 = f32[4,16,16,4]{3,2,1,0:T(8,128)S(1)} collective-permute-done((f32[4,16,16,4]{3,2,1,0:T(8,128)}, f32[4,16,16,4]{3,2,1,0:T(8,128)S(1)}, u32[]{:S(2)}, u32[]{:S(2)}) %collective-permute-start.15) | collective-permute-done | bytes 16416 | tf_op jit(solution)/shard_map/ppermute | solution.py:38
  178.7 1.7 broadcast_multiply_fusion
  184.1 5.0 %sample.1 = f32[48,128]{1,0:T(8,128)} custom-call(f32[384,128]{1,0:T(8,128)} %bitcast.69, f32[96,128]{1,0:T(8,128)} %get-tuple-element.6.state_ref), custom_call_target="tpu_custom_call" | custom-call | tf_op jit(solution)/shard_map/sample/pallas_call | solution.py:349
  190.5 3.4 %all-to-all-start.2 = ((f32[16,1,384]{2,1,0:T(1,128)}), f32[16,1,384]{2,1,0:T(1,128)S(1)}, u32[]{:S(2)}, u32[]{:S(2)}) async-start(f32[16,1,384]{2,1,0:T(1,128)} %all_to_all.26), calls=%async_computation.2 | async-start | bytes 49152 | tf_op jit(solution)/shard_map/all_to_all | solution.py:474
  194.5 3.5 %all-to-all-done.2 = f32[16,1,384]{2,1,0:T(1,128)S(1)} async-done(((f32[16,1,384]{2,1,0:T(1,128)}), f32[16,1,384]{2,1,0:T(1,128)S(1)}, u32[]{:S(2)}, u32[]{:S(2)}) %all-to-all-start.2) | async-done | bytes 24608 | tf_op jit(solution)/shard_map/all_to_all | solution.py:474
  (156 shorter events, 32.7 us)
Async XLA Ops:
  0.6 26.8 %copy-start.21 = (f32[8,8,128]{2,1,0:T(8,128)S(1)}, f32[8,8,128]{2,1,0:T(8,128)}, u32[]{:S(2)}) copy-start(f32[8,8,128]{2,1,0:T(8,128)} %param.11) | copy-start | bytes 98308
  0.6 26.8 %copy-start.5 = (f32[3,8,8,128]{3,2,1,0:T(8,128)S(1)}, f32[3,8,8,128]{3,2,1,0:T(8,128)}, u32[]{:S(2)}) copy-start(f32[3,8,8,128]{3,2,1,0:T(8,128)} %param.10) | copy-start | bytes 294916
  3.1 16.8 %all-to-all-start = ((f32[16,1,1792]{2,1,0:T(1,128)}), f32[16,1,1792]{2,1,0:T(1,128)S(1)}, u32[]{:S(2)}, u32[]{:S(2)}) async-start(f32[16,1,1792]{2,1,0:T(1,128)} %all_to_all.24), calls=%async_computation | async-start | bytes 229376 | tf_op jit(solution)/shard_map/all_to_all | solution.py:444
  11.4 16.0 %collective-permute-start.16 = (f32[4,8,5,128]{3,2,1,0:T(8,128)S(1)}, f32[4,8,5,128]{3,2,1,0:T(8,128)S(1)}, u32[]{:S(2)}, u32[]{:S(2)}) collective-permute-start(f32[4,8,5,128]{3,2,1,0:T(8,128)S(1)} %get-tuple-element.48), channel_id=1, source_target_pairs={{0,16},{16,32},{32,48},{1,17},{17,33},{33,49},{2,18},{18,34},{34,5... | collective-permute-start | bytes 245768 | tf_op jit(solution)/shard_map/ppermute | solution.py:37
  16.3 11.1 %collective-permute-start.17 = (f32[4,8,5,128]{3,2,1,0:T(8,128)S(1)}, f32[4,8,5,128]{3,2,1,0:T(8,128)S(1)}, u32[]{:S(2)}, u32[]{:S(2)}) collective-permute-start(f32[4,8,5,128]{3,2,1,0:T(8,128)S(1)} %get-tuple-element.49), channel_id=1, source_target_pairs={{16,0},{32,16},{48,32},{17,1},{33,17},{49,33},{18,2},{34,18},{50,3... | collective-permute-start | bytes 245768 | tf_op jit(solution)/shard_map/ppermute | solution.py:38
  20.3 22.8 %copy-start.4 = (f32[126,128]{1,0:T(8,128)}, f32[126,128]{1,0:T(8,128)S(1)}, u32[]{:S(2)}) copy-start(f32[126,128]{1,0:T(8,128)S(1)} %reshape.115.refs_0_.refs_5_) | copy-start | bytes 193540
  20.3 7.3 %collective-permute-start = (f32[126,128]{1,0:T(8,128)S(1)}, f32[126,128]{1,0:T(8,128)S(1)}, u32[]{:S(2)}, u32[]{:S(2)}) collective-permute-start(f32[126,128]{1,0:T(8,128)S(1)} %reshape.115.refs_0_.refs_5_), channel_id=1, source_target_pairs={{0,16},{16,32},{32,48},{1,17},{17,33},{33,49},{2,18},{18,34},{34,5... | collective-permute-start | bytes 193544 | tf_op jit(solution)/shard_map/ppermute | solution.py:37
  26.1 7.1 %collective-permute-start.1 = (f32[126,128]{1,0:T(8,128)S(1)}, f32[126,128]{1,0:T(8,128)S(1)}, u32[]{:S(2)}, u32[]{:S(2)}) collective-permute-start(f32[126,128]{1,0:T(8,128)S(1)} %reshape.115.refs_0_.refs_5_), channel_id=1, source_target_pairs={{16,0},{32,16},{48,32},{17,1},{33,17},{49,33},{18,2},{34,18},{50,3... | collective-permute-start | bytes 193544 | tf_op jit(solution)/shard_map/ppermute | solution.py:38
  27.4 60.2 %copy-start.8 = (f32[4,8,5,128]{3,2,1,0:T(8,128)}, f32[4,8,5,128]{3,2,1,0:T(8,128)S(1)}, u32[]{:S(2)}) copy-start(f32[4,8,5,128]{3,2,1,0:T(8,128)S(1)} %collective-permute-done.16) | copy-start | bytes 245764
  27.5 60.2 %copy-start.9 = (f32[4,8,5,128]{3,2,1,0:T(8,128)}, f32[4,8,5,128]{3,2,1,0:T(8,128)S(1)}, u32[]{:S(2)}) copy-start(f32[4,8,5,128]{3,2,1,0:T(8,128)S(1)} %collective-permute-done.17) | copy-start | bytes 245764
  33.3 9.8 %collective-permute-start.2 = (f32[378,128]{1,0:T(8,128)S(1)}, f32[378,128]{1,0:T(8,128)S(1)}, u32[]{:S(2)}, u32[]{:S(2)}) collective-permute-start(f32[378,128]{1,0:T(8,128)S(1)} %pad_maximum_fusion.12), channel_id=1, source_target_pairs={{0,64},{64,128},{128,192},{1,65},{65,129},{129,193},{2,66},{66,130... | collective-permute-start | bytes 580616 | tf_op jit(solution)/shard_map/ppermute | solution.py:37
  36.4 6.7 %collective-permute-start.3 = (f32[378,128]{1,0:T(8,128)S(1)}, f32[378,128]{1,0:T(8,128)S(1)}, u32[]{:S(2)}, u32[]{:S(2)}) collective-permute-start(f32[378,128]{1,0:T(8,128)S(1)} %pad_maximum_fusion.12), channel_id=1, source_target_pairs={{64,0},{128,64},{192,128},{65,1},{129,65},{193,129},{66,2},{130,66... | collective-permute-start | bytes 580616 | tf_op jit(solution)/shard_map/ppermute | solution.py:38
  37.8 49.9 %collective-permute-start.18 = (f32[4,5,18,128]{3,2,1,0:T(8,128)S(1)}, f32[4,5,18,128]{3,2,1,0:T(8,128)S(1)}, u32[]{:S(2)}, u32[]{:S(2)}) collective-permute-start(f32[4,5,18,128]{3,2,1,0:T(8,128)S(1)} %get-tuple-element.36), channel_id=1, source_target_pairs={{0,64},{64,128},{128,192},{1,65},{65,129},{129,193},{2,66},{66,130... | collective-permute-start | bytes 552968 | tf_op jit(solution)/shard_map/ppermute | solution.py:37
  41.8 45.9 %collective-permute-start.19 = (f32[4,5,18,128]{3,2,1,0:T(8,128)S(1)}, f32[4,5,18,128]{3,2,1,0:T(8,128)S(1)}, u32[]{:S(2)}, u32[]{:S(2)}) collective-permute-start(f32[4,5,18,128]{3,2,1,0:T(8,128)S(1)} %get-tuple-element.37), channel_id=1, source_target_pairs={{64,0},{128,64},{192,128},{65,1},{129,65},{193,129},{66,2},{130,66... | collective-permute-start | bytes 552968 | tf_op jit(solution)/shard_map/ppermute | solution.py:38
  67.2 9.1 %collective-permute-start.4 = (f32[6,1,128]{2,1,0:T(1,128)S(1)}, f32[6,1,128]{2,1,0:T(1,128)S(1)}, u32[]{:S(2)}, u32[]{:S(2)}) collective-permute-start(f32[6,1,128]{2,1,0:T(1,128)S(1)} %get-tuple-element.56), channel_id=1, source_target_pairs={{0,1},{1,2},{2,3},{3,4},{4,5},{5,6},{6,7},{7,8},{8,9},{9,10},{10,1... | collective-permute-start | bytes 9224 | tf_op jit(solution)/shard_map/ppermute | solution.py:37
  73.9 4.9 %collective-permute-start.5 = (f32[6,1,128]{2,1,0:T(1,128)S(1)}, f32[6,1,128]{2,1,0:T(1,128)S(1)}, u32[]{:S(2)}, u32[]{:S(2)}) collective-permute-start(f32[6,1,128]{2,1,0:T(1,128)S(1)} %get-tuple-element.57), channel_id=1, source_target_pairs={{1,0},{2,1},{3,2},{4,3},{5,4},{6,5},{7,6},{8,7},{9,8},{10,9},{11,1... | collective-permute-start | bytes 9224 | tf_op jit(solution)/shard_map/ppermute | solution.py:38
  79.7 19.1 %copy-start.22 = (f32[108,128]{1,0:T(8,128)}, f32[108,128]{1,0:T(8,128)S(1)}, u32[]{:S(2)}) copy-start(f32[108,128]{1,0:T(8,128)S(1)} %reshape.117.refs_0_) | copy-start | bytes 165892
  79.7 8.1 %collective-permute-start.6 = (f32[108,128]{1,0:T(8,128)S(1)}, f32[108,128]{1,0:T(8,128)S(1)}, u32[]{:S(2)}, u32[]{:S(2)}) collective-permute-start(f32[108,128]{1,0:T(8,128)S(1)} %reshape.117.refs_0_), channel_id=1, source_target_pairs={{0,16},{16,32},{32,48},{1,17},{17,33},{33,49},{2,18},{18,34},{34,5... | collective-permute-start | bytes 165896 | tf_op jit(solution)/shard_map/ppermute | solution.py:37
  86.3 5.8 %collective-permute-start.7 = (f32[108,128]{1,0:T(8,128)S(1)}, f32[108,128]{1,0:T(8,128)S(1)}, u32[]{:S(2)}, u32[]{:S(2)}) collective-permute-start(f32[108,128]{1,0:T(8,128)S(1)} %reshape.117.refs_0_), channel_id=1, source_target_pairs={{16,0},{32,16},{48,32},{17,1},{33,17},{49,33},{18,2},{34,18},{50,3... | collective-permute-start | bytes 165896 | tf_op jit(solution)/shard_map/ppermute | solution.py:38
  92.8 19.1 %collective-permute-start.8 = (f32[324,128]{1,0:T(8,128)}, f32[324,128]{1,0:T(8,128)}, u32[]{:S(2)}, u32[]{:S(2)}) collective-permute-start(f32[324,128]{1,0:T(8,128)} %pad_maximum_fusion.14), channel_id=1, source_target_pairs={{0,64},{64,128},{128,192},{1,65},{65,129},{129,193},{2,66},{66,130... | collective-permute-start | bytes 497672 | tf_op jit(solution)/shard_map/ppermute | solution.py:37
  98.8 13.2 %collective-permute-start.9 = (f32[324,128]{1,0:T(8,128)}, f32[324,128]{1,0:T(8,128)}, u32[]{:S(2)}, u32[]{:S(2)}) collective-permute-start(f32[324,128]{1,0:T(8,128)} %pad_maximum_fusion.14), channel_id=1, source_target_pairs={{64,0},{128,64},{192,128},{65,1},{129,65},{193,129},{66,2},{130,66... | collective-permute-start | bytes 497672 | tf_op jit(solution)/shard_map/ppermute | solution.py:38
  100.9 6.0 %collective-permute-start.20 = (f32[4,18,18,5]{2,0,3,1:T(4,128)S(1)}, f32[4,18,18,5]{2,0,3,1:T(4,128)S(1)}, u32[]{:S(2)}, u32[]{:S(2)}) collective-permute-start(f32[4,18,18,5]{2,0,3,1:T(4,128)S(1)} %copy.45), channel_id=1, source_target_pairs={{0,1},{1,2},{2,3},{3,4},{4,5},{5,6},{6,7},{7,8},{8,9},{9,10},{10,1... | collective-permute-start | bytes 77768 | tf_op jit(solution)/shard_map/ppermute | solution.py:37
  104.5 6.9 %collective-permute-start.21 = (f32[4,18,18,5]{2,0,3,1:T(4,128)S(1)}, f32[4,18,18,5]{2,0,3,1:T(4,128)S(1)}, u32[]{:S(2)}, u32[]{:S(2)}) collective-permute-start(f32[4,18,18,5]{2,0,3,1:T(4,128)S(1)} %copy.46), channel_id=1, source_target_pairs={{1,0},{2,1},{3,2},{4,3},{5,4},{6,5},{7,6},{8,7},{9,8},{10,9},{11,1... | collective-permute-start | bytes 77768 | tf_op jit(solution)/shard_map/ppermute | solution.py:38
  138.2 7.1 %collective-permute-start.10 = (f32[4,8,4,128]{3,2,1,0:T(4,128)S(1)}, f32[4,8,4,128]{3,2,1,0:T(4,128)S(1)}, u32[]{:S(2)}, u32[]{:S(2)}) collective-permute-start(f32[4,8,4,128]{3,2,1,0:T(4,128)S(1)} %get-tuple-element.46), channel_id=1, source_target_pairs={{0,16},{16,32},{32,48},{1,17},{17,33},{33,49},{2,18},{18,34},{34,5... | collective-permute-start | bytes 196616 | tf_op jit(solution)/shard_map/ppermute | solution.py:37
  141.7 6.0 %collective-permute-start.11 = (f32[4,8,4,128]{3,2,1,0:T(4,128)S(1)}, f32[4,8,4,128]{3,2,1,0:T(4,128)S(1)}, u32[]{:S(2)}, u32[]{:S(2)}) collective-permute-start(f32[4,8,4,128]{3,2,1,0:T(4,128)S(1)} %get-tuple-element.47), channel_id=1, source_target_pairs={{16,0},{32,16},{48,32},{17,1},{33,17},{49,33},{18,2},{34,18},{50,3... | collective-permute-start | bytes 196616 | tf_op jit(solution)/shard_map/ppermute | solution.py:38
  147.8 9.0 %collective-permute-start.12 = (f32[4,4,16,128]{3,2,1,0:T(8,128)S(1)}, f32[4,4,16,128]{3,2,1,0:T(8,128)S(1)}, u32[]{:S(2)}, u32[]{:S(2)}) collective-permute-start(f32[4,4,16,128]{3,2,1,0:T(8,128)S(1)} %get-tuple-element.40), channel_id=1, source_target_pairs={{0,64},{64,128},{128,192},{1,65},{65,129},{129,193},{2,66},{66,130... | collective-permute-start | bytes 393224 | tf_op jit(solution)/shard_map/ppermute | solution.py:37
  154.4 5.7 %collective-permute-start.13 = (f32[4,4,16,128]{3,2,1,0:T(8,128)S(1)}, f32[4,4,16,128]{3,2,1,0:T(8,128)S(1)}, u32[]{:S(2)}, u32[]{:S(2)}) collective-permute-start(f32[4,4,16,128]{3,2,1,0:T(8,128)S(1)} %get-tuple-element.41), channel_id=1, source_target_pairs={{64,0},{128,64},{192,128},{65,1},{129,65},{193,129},{66,2},{130,66... | collective-permute-start | bytes 393224 | tf_op jit(solution)/shard_map/ppermute | solution.py:38
  160.2 17.3 %copy-start.1 = (f32[256,128]{1,0:T(8,128)S(1)}, f32[256,128]{1,0:T(8,128)}, u32[]{:S(2)}) copy-start(f32[256,128]{1,0:T(8,128)} %get-tuple-element.7) | copy-start | bytes 393220
  161.4 10.0 %collective-permute-start.14 = (f32[4,16,16,4]{3,2,1,0:T(8,128)}, f32[4,16,16,4]{3,2,1,0:T(8,128)S(1)}, u32[]{:S(2)}, u32[]{:S(2)}) collective-permute-start(f32[4,16,16,4]{3,2,1,0:T(8,128)} %get-tuple-element.34), channel_id=1, source_target_pairs={{0,1},{1,2},{2,3},{3,4},{4,5},{5,6},{6,7},{7,8},{8,9},{9,10},{10,1... | collective-permute-start | bytes 49160 | tf_op jit(solution)/shard_map/ppermute | solution.py:37
  165.0 12.6 %collective-permute-start.15 = (f32[4,16,16,4]{3,2,1,0:T(8,128)}, f32[4,16,16,4]{3,2,1,0:T(8,128)S(1)}, u32[]{:S(2)}, u32[]{:S(2)}) collective-permute-start(f32[4,16,16,4]{3,2,1,0:T(8,128)} %get-tuple-element.35), channel_id=1, source_target_pairs={{1,0},{2,1},{3,2},{4,3},{5,4},{6,5},{7,6},{8,7},{9,8},{10,9},{11,1... | collective-permute-start | bytes 49160 | tf_op jit(solution)/shard_map/ppermute | solution.py:38
  167.6 22.8 %all-to-all-start.1 = ((f32[16,1,384]{2,1,0:T(1,128)}), f32[16,1,384]{2,1,0:T(1,128)S(1)}, u32[]{:S(2)}, u32[]{:S(2)}) async-start(f32[16,1,384]{2,1,0:T(1,128)} %all_to_all.25), calls=%async_computation.1 | async-start | bytes 49152 | tf_op jit(solution)/shard_map/all_to_all | solution.py:474
  190.5 7.6 %all-to-all-start.2 = ((f32[16,1,384]{2,1,0:T(1,128)}), f32[16,1,384]{2,1,0:T(1,128)S(1)}, u32[]{:S(2)}, u32[]{:S(2)}) async-start(f32[16,1,384]{2,1,0:T(1,128)} %all_to_all.26), calls=%async_computation.2 | async-start | bytes 49152 | tf_op jit(solution)/shard_map/all_to_all | solution.py:474
  (29 other events, 186.8 us)
where the time goes:
time: 199 us
  starting transfers between devices  84.3 us (42%)
  Pallas kernels  52.3 us (26%)
  waiting for transfers between devices  31.9 us (16%)
  other arithmetic  17.4 us (9%)
  local copies, waits for them, and re-layouts  11.3 us (6%)
    ppermute x11, starting transfers between devices, shift_pair(): from_below = lax.ppermute(array_high, axis, forward)  53.8 us
    pallas_call x2, Pallas kernels, contact(): pl.pallas_call(lambda *refs: contact_kernel(deposit, *refs), out_shape=sh...  47.3 us
    ppermute x11, waiting for transfers between devices, shift_pair(): from_above = lax.ppermute(array_low, axis, backward)  28.2 us
    ppermute x11, starting transfers between devices, shift_pair(): from_above = lax.ppermute(array_low, axis, backward)  16.2 us
    all_to_all x1, starting transfers between devices, body(): got = lax.all_to_all(sent, 'gz', split_axis=0, concat_axis=0, tiled=True)  7.33 us
    all_to_all x2, starting transfers between devices, back(): lax.all_to_all(sent_back, 'gz', split_axis=0, concat_axis=0, tiled=True)  6.95 us
    pallas_call x1, Pallas kernels, sample(): pl.pallas_call(sample_kernel, out_shape=jax.ShapeDtypeStruct((48, S), jnp...  5 us
  transfers between devices with their start and end apart: 25, of which 9 were waited for; matrix products, arithmetic and copies ran while one was open for 10% of the time, Pallas kernels for 14%

commit v1 on v0

v1 whole, which is shorter than its diff:
```python
import math

import jax
import jax.numpy as jnp
from jax import lax
from jax.experimental import pallas as pl
from jax.experimental.pallas import tpu as pltpu
from jax.sharding import PartitionSpec as P

B = 8
S = 128
PZ = 16
SWEEPS = 3
DAMPING = 0.5
TIME_STEP = 0.005
GRAVITY = 1.0
SOFTENING = 0.0025
GAS_STEP = 0.2
GAS_DRAG = 2.0
PARTICLE_DRAG = 4.0
COUPLE_STEP = 0.25
LOWER_BOUND = 0.2
UPPER_BOUND = 2.0

REACH = 0.194
FAR = 1e30
NEAR = tuple((dx, dy, dz) for dx in (-1, 0, 1) for dy in (-1, 0, 1) for dz in (-1, 0, 1))
HIGHEST = lax.Precision.HIGHEST

L0 = PZ + 6
L1 = PZ + 4
L2 = PZ + 2
RADIUS_ROW = 6 * L0
WG = 5
WD = 4


def shift_pair(array_low, array_high, axis):
    count = lax.axis_size(axis)
    forward = [(i, i + 1) for i in range(count - 1)]
    backward = [(i + 1, i) for i in range(count - 1)]
    from_below = lax.ppermute(array_high, axis, forward)
    from_above = lax.ppermute(array_low, axis, backward)
    return from_below, from_above


def chebyshev_factor(sweep_index, sweeps):
    centre = 0.5 * (UPPER_BOUND + LOWER_BOUND)
    radius_half = 0.5 * (UPPER_BOUND - LOWER_BOUND)
    return 1.0 / (centre + radius_half * math.cos(math.pi * (2 * sweep_index + 1) / (2 * sweeps)))


def lane_iota(rows):
    return lax.broadcasted_iota(jnp.int32, (rows, S), 1)


def axis_weights(row):
    centres = lax.broadcasted_iota(jnp.int32, (B, S), 0).astype(jnp.float32) + 0.5
    gap = jnp.broadcast_to(row, (B, S)) * float(B) - centres
    kernel = jnp.exp(-gap * gap)
    return kernel / jnp.sum(kernel, axis=0, keepdims=True)


def plane_weights(row_x, row_y):
    wx = axis_weights(row_x)
    wy = axis_weights(row_y)
    return jnp.concatenate(
        [jnp.broadcast_to(wx[a : a + 1], (B, S)) * wy for a in range(B)], axis=0
    )


def contact_kernel(cells, deposit, *refs):
    p_own, p_ylo, p_yhi, p_xlo, p_xhi, r_own, r_ylo, r_yhi, r_xlo, r_xhi = refs[:10]
    out_ref = refs[10]
    rest = refs[11:]
    if deposit:
        dep_ref, dep_lo_ref, dep_hi_ref = rest[:3]
        rest = rest[3:]
    mask_s, pref_s, work_s, key_s, list_s, own_s, cell_s, acc_s, force_s, rows_s, slots_s = rest[:11]
    layers = cells + 2
    shift = (L0 - cells) // 2
    block = 7 * L0 if cells == L1 else 6 * L1

    def source(dx, dy):
        if dx == 0:
            return ((p_ylo, p_own, p_yhi)[dy + 1], 0, (r_ylo, r_own, r_yhi)[dy + 1], RADIUS_ROW)
        p_ref, r_ref = (p_xlo, r_xlo) if dx < 0 else (p_xhi, r_xhi)
        return p_ref, (dy + 1) * block, r_ref, (dy + 1) * 7 * L0 + RADIUS_ROW

    lane = lane_iota(8)
    tri_row = lax.broadcasted_iota(jnp.int32, (S, 2 * S), 0)
    tri_col = lax.broadcasted_iota(jnp.int32, (S, 2 * S), 1)
    tri = jnp.where((tri_row < tri_col) | (tri_col >= S), 1.0, 0.0).astype(jnp.bfloat16)

    for start in (0, 8, cells - 8):
        own_r = r_own[RADIUS_ROW + shift + start : RADIUS_ROW + shift + start + 8, :]
        own_live = own_r > 0.0
        bounds = []
        for f in range(3):
            first = f * layers + 1 + start
            value = p_own[first : first + 8, :]
            top = jnp.max(jnp.where(own_live, value, -FAR), axis=1, keepdims=True) + REACH
            bottom = jnp.min(jnp.where(own_live, value, FAR), axis=1, keepdims=True) - REACH
            bounds.append((jnp.broadcast_to(bottom, (8, S)), jnp.broadcast_to(top, (8, S))))
        used = jnp.max(
            jnp.where(own_live, (lane + 1).astype(jnp.float32), 0.0), axis=1, keepdims=True
        )
        for k, offset in enumerate(NEAR):
            p_ref, p_base, r_ref, r_base = source(offset[0], offset[1])
            row = r_base + shift + start + offset[2]
            keep = r_ref[row : row + 8, :] > 0.0
            for f in range(3):
                row = p_base + f * layers + 1 + start + offset[2]
                value = p_ref[row : row + 8, :] + float(offset[f])
                keep = keep & (value >= bounds[f][0]) & (value <= bounds[f][1])
            mask_s[k * 8 : k * 8 + 8, :] = jnp.where(keep, 1.0, 0.0)
        pref_s[...] = jnp.dot(
            mask_s[...].astype(jnp.bfloat16), tri, preferred_element_type=jnp.float32
        )
        base = jnp.zeros((8, S), jnp.int32)
        for k, offset in enumerate(NEAR):
            before = pref_s[k * 8 : k * 8 + 8, 0:S].astype(jnp.int32)
            count = pref_s[k * 8 : k * 8 + 8, S : 2 * S].astype(jnp.int32)
            hop = jnp.where(mask_s[k * 8 : k * 8 + 8, :] > 0.0, lane - before, 0)
            for bit in range(7):
                step = 1 << bit
                moved = pltpu.roll(hop, S - step, 1)
                hop = jnp.where(
                    (moved & step) != 0, moved, jnp.where((hop & step) != 0, 0, hop)
                )
            slot = (lane - base) & (S - 1)
            pick = (jnp.take_along_axis(hop, slot, axis=1) + slot) & (S - 1)
            page = (base >> 7) + jnp.where(lane < (base & (S - 1)), 1, 0)
            key_s[k * 8 : k * 8 + 8, :] = jnp.where(slot < count, page, -1)
            base = base + count
            p_ref, p_base, r_ref, r_base = source(offset[0], offset[1])
            for f in range(7):
                if f < 6:
                    row = p_base + f * layers + 1 + start + offset[2]
                    value = p_ref[row : row + 8, :]
                    if f < 3 and offset[f] != 0:
                        value = value + float(offset[f])
                else:
                    row = r_base + shift + start + offset[2]
                    value = r_ref[row : row + 8, :]
                work_s[k, f] = jnp.take_along_axis(value, pick, axis=1)
        total = base.astype(jnp.float32)
        pages = (jnp.max(total).astype(jnp.int32) + (S - 1)) >> 7
        for i in range(8):
            rows_s[start + i] = (
                jnp.max(total[i : i + 1, :]).astype(jnp.int32) + (S - 1)
            ) >> 7
            slots_s[start + i] = jnp.max(used[i : i + 1, :]).astype(jnp.int32)

        def merge(page, carry):
            acc = [jnp.zeros((8, S), jnp.float32)] * 6 + [jnp.full((8, S), -10.0, jnp.float32)]
            for k in range(27):
                here = key_s[k * 8 : k * 8 + 8, :] == page
                acc = [jnp.where(here, work_s[k, f], acc[f]) for f in range(7)]
            for f in range(7):
                list_s[page, f, start : start + 8, :] = acc[f]
            return carry

        lax.fori_loop(0, pages, merge, 0)

    radius = r_own[RADIUS_ROW + shift : RADIUS_ROW + shift + cells, :]
    live = radius > 0.0
    own_s[...] = jnp.zeros((2 * S, S), jnp.float32)
    for f in range(6):
        own_s[f * 32 : f * 32 + cells, :] = p_own[f * layers + 1 : f * layers + 1 + cells, :]
    own_s[6 * 32 : 6 * 32 + cells, :] = jnp.where(live, radius, -10.0)
    turned = (own_s[0:S, :].T, own_s[S : 2 * S, :].T)
    own_s[0:S, :] = turned[0]
    own_s[S : 2 * S, :] = turned[1]
    force_s[...] = jnp.zeros((S, S), jnp.float32)

    def cell_forces(cell, page_count, tiles):
        for t in range(tiles):
            for f in range(7):
                tile = own_s[(f // 4) * S + 8 * t : (f // 4) * S + 8 * t + 8, :]
                cell_s[t, f] = jnp.take_along_axis(
                    tile, jnp.full((8, S), (f % 4) * 32, jnp.int32) + cell, axis=1
                )

        def near_page(page, fresh):
            near = [
                jnp.broadcast_to(list_s[page, f, pl.ds(cell, 1), :], (8, S)) for f in range(7)
            ]
            for t in range(tiles):
                ex = near[0] - cell_s[t, 0]
                ey = near[1] - cell_s[t, 1]
                ez = near[2] - cell_s[t, 2]
                square = ex * ex + ey * ey + ez * ez + SOFTENING
                inverse = lax.rsqrt(square)
                press = jnp.maximum((near[6] + cell_s[t, 6]) - square * inverse, 0.0)
                closing = (
                    (near[3] - cell_s[t, 3]) * ex
                    + (near[4] - cell_s[t, 4]) * ey
                    + (near[5] - cell_s[t, 5]) * ez
                )
                size = press * inverse * (1.0 - DAMPING * (closing * inverse))
                for f, part in enumerate((size * ex, size * ey, size * ez)):
                    acc_s[t, f] = part if fresh else acc_s[t, f] + part

        near_page(0, True)

        def more(page, carry):
            near_page(page, False)
            return carry

        lax.fori_loop(1, page_count, more, 0)
        for t in range(tiles):
            rows = slice(8 * t, 8 * t + 8)
            tile = force_s[rows, :]
            for f in range(3):
                total_f = jnp.sum(acc_s[t, f], axis=1, keepdims=True)
                tile = jnp.where(
                    lane == f * 32 + cell, jnp.broadcast_to(total_f, (8, S)), tile
                )
            force_s[rows, :] = tile

    def one_cell(cell, carry):
        page_count = rows_s[cell]
        slot_count = slots_s[cell]
        for tiles in (4, 8, 12, 16):

            @pl.when((slot_count > 8 * tiles - 32) & (slot_count <= 8 * tiles))
            def _():
                cell_forces(cell, page_count, tiles)

        return carry

    lax.fori_loop(0, cells, one_cell, 0)

    force = force_s[...].T
    scale = jnp.where(live, -1.0 / (radius * radius * radius), 0.0)
    for f in range(3):
        push = force[f * 32 : f * 32 + cells, :] * scale
        if f == 2:
            push = push - GRAVITY
        first = (3 + f) * layers + 1
        speed = p_own[first : first + cells, :] + TIME_STEP * push
        first = f * layers + 1
        place = p_own[first : first + cells, :] + TIME_STEP * speed
        out_ref[f * cells : f * cells + cells, :] = place
        out_ref[(3 + f) * cells : (3 + f) * cells + cells, :] = speed

    if deposit:
        dep_s, edge_s = rest[11:13]

        def one_deposit(cell):
            def row(f):
                return out_ref[pl.ds(f * cells + cell, 1), :]

            r = r_own[pl.ds(RADIUS_ROW + shift + cell, 1), :]
            volume = (4.0 * math.pi / 3.0 * B**3) * (r * r * r)
            plane = plane_weights(row(0), row(1))
            wz = axis_weights(row(2))
            carried = [volume, volume * row(3), volume * row(4), volume * row(5)]
            left = jnp.concatenate(
                [jnp.broadcast_to(c, (B, S)) * wz for c in carried], axis=0
            )
            return lax.dot_general(
                left,
                plane,
                (((1,), (1,)), ((), ())),
                precision=HIGHEST,
                preferred_element_type=jnp.float32,
            )

        def some_deposits(step, carry):
            blocks = [one_deposit(step * 3 + i) for i in range(3)]
            for i in range(3):
                for f in range(4):
                    dep_s[f, pl.ds(pl.multiple_of(step * 24 + i * 8, 8), 8), 0:64] = blocks[i][
                        f * 8 : f * 8 + 8, :
                    ]
            return carry

        lax.fori_loop(0, cells // 3, some_deposits, 0)
        edge_s[...] = jnp.zeros((S, S), jnp.float32)
        for f in range(4):
            edge_s[f * 32 : f * 32 + 8, :] = dep_s[f, B + S : B + S + 8, :]
            edge_s[f * 32 + 24 : f * 32 + 32, :] = dep_s[f, 0:B, :]
        for f in range(5):
            grid = (dep_s[f, B : B + S, :] if f < 4 else edge_s[...]).T
            dep_ref[f * 64 : f * 64 + 64, :] = grid[0:64, :]
            for x in range(B):
                row = (f * B + x) * WD
                dep_lo_ref[row : row + WD, :] = grid[x * B : x * B + WD, :]
                dep_hi_ref[row : row + WD, :] = grid[x * B + B - WD : x * B + B, :]


def contact(cells, deposit, places, radii):
    shapes = [jax.ShapeDtypeStruct((6 * cells, S), jnp.float32)]
    scratch = [
        pltpu.VMEM((27 * 8, S), jnp.float32),
        pltpu.VMEM((27 * 8, 2 * S), jnp.float32),
        pltpu.VMEM((27, 7, 8, S), jnp.float32),
        pltpu.VMEM((27 * 8, S), jnp.int32),
        pltpu.VMEM((27, 7, 24, S), jnp.float32),
        pltpu.VMEM((2 * S, S), jnp.float32),
        pltpu.VMEM((16, 7, 8, S), jnp.float32),
        pltpu.VMEM((16, 3, 8, S), jnp.float32),
        pltpu.VMEM((S, S), jnp.float32),
        pltpu.SMEM((24,), jnp.int32),
        pltpu.SMEM((24,), jnp.int32),
    ]
    if deposit:
        shapes.append(jax.ShapeDtypeStruct((5 * 64, S), jnp.float32))
        shapes += [jax.ShapeDtypeStruct((5 * B * WD, S), jnp.float32)] * 2
        scratch += [pltpu.VMEM((4, S + 2 * B, S), jnp.float32), pltpu.VMEM((S, S), jnp.float32)]
    return pl.pallas_call(
        lambda *refs: contact_kernel(cells, deposit, *refs),
        out_shape=shapes,
        scratch_shapes=scratch,
        name="contact_deposit" if deposit else "contact",
    )(*places, *radii)


def assemble(target, edge, own, ylo, yhi, xlo, xhi, y_at, x_at, width):
    span = B + 2 * width

    def put(field, x, y, value):
        rows = slice(y, y + value.shape[0])
        if field < 4:
            target[field, x, rows, 0:S] = value
        else:
            edge[x, rows, :] = value

    for field in range(5):
        for x in range(B):
            row = (field * B + x) * B
            put(field, width + x, width, own[row : row + B, :])
            row = y_at + (field * B + x) * width
            put(field, width + x, 0, ylo[row : row + width, :])
            put(field, width + x, width + B, yhi[row : row + width, :])
        for x in range(width):
            for place, ref in ((x, xlo), (width + B + x, xhi)):
                row = x_at + (field * width + x) * B
                put(field, place, width, ref[row : row + B, :])
                row = x_at + 5 * width * B + (field * width + x) * width
                put(field, place, 0, ref[row : row + width, :])
                row += 5 * width * width
                put(field, place, width + B, ref[row : row + width, :])
    lane = lane_iota(8)
    for field in range(4):
        index = field * 32 + jnp.where(
            lane < 64, jnp.minimum(lane, 15), jnp.maximum(lane - 96, 16)
        )
        for x in range(span):
            for y in range(0, edge.shape[1], 8):
                target[field, x, y : y + 8, S : 2 * S] = jnp.take_along_axis(
                    edge[x, y : y + 8, :], index, axis=1
                )


def gas_kernel(*refs):
    (
        rank_ref,
        g_own,
        g_ylo,
        g_yhi,
        g_xlo,
        g_xhi,
        d_own,
        d_ylo,
        d_yhi,
        d_xlo,
        d_xhi,
        state_ref,
        sent_ref,
        newv_ref,
        newp_ref,
        u_s,
        ue_s,
        d_s,
        de_s,
        flux_s,
        mid_s,
        inv_s,
        src_s,
        pa_s,
        pb_s,
        grad_s,
        field_s,
        pair_s,
        sum_s,
    ) = refs
    assemble(u_s, ue_s, g_own, g_ylo, g_yhi, g_xlo, g_xhi, 6 * L1, 18 * L1, WG)
    assemble(d_s, de_s, d_own, d_ylo, d_yhi, d_xlo, d_xhi, 0, 0, WD)
    wide = B + 2 * WD
    ring = 2 * S

    def zdiff(value):
        return pltpu.roll(value, ring - 1, 1) - pltpu.roll(value, 1, 1)

    def zsum(value):
        return pltpu.roll(value, ring - 1, 1) + pltpu.roll(value, 1, 1)

    def ydiff(value):
        return pltpu.roll(value, wide - 1, 0) - pltpu.roll(value, 1, 0)

    def ysum(value):
        return pltpu.roll(value, wide - 1, 0) + pltpu.roll(value, 1, 0)

    for x in range(wide):
        speed = [u_s[d, x + 1, 1 : wide + 1, :] for d in range(3)]
        solids = d_s[0, x]
        voidage = 1.0 / (1.0 + solids)
        under = 1.0 / (voidage + GAS_STEP * GAS_DRAG * solids)
        inv_s[x] = 1.0 / (6.0 + voidage)
        for k in range(3):
            slope = speed[0] * (u_s[k, x + 2, 1 : wide + 1, :] - u_s[k, x, 1 : wide + 1, :])
            slope += speed[1] * (u_s[k, x + 1, 2 : wide + 2, :] - u_s[k, x + 1, 0:wide, :])
            slope += speed[2] * zdiff(speed[k])
            pulled = speed[k] - (0.5 * GAS_STEP) * slope
            middle = (voidage * pulled + GAS_STEP * GAS_DRAG * d_s[1 + k, x]) * under
            mid_s[k, x] = middle
            flux_s[k, x] = voidage * middle
        pa_s[x] = u_s[3, x + 1, 1 : wide + 1, :]
    for x in range(1, wide - 1):
        spread = (flux_s[0, x + 1] - flux_s[0, x - 1]) + ydiff(flux_s[1, x]) + zdiff(flux_s[2, x])
        src_s[x] = (-0.5 / GAS_STEP) * spread * inv_s[x]

    row = lax.broadcasted_iota(jnp.int32, (wide, ring), 0) - WD + rank_ref[1] * B
    col = lax.broadcasted_iota(jnp.int32, (wide, ring), 1)
    col = jnp.where(col < ring - 64, col, col - ring) + rank_ref[2] * S
    inside = (row >= 0) & (row < rank_ref[4]) & (col >= 0) & (col < rank_ref[5])
    for sweep in range(SWEEPS):
        old, new = (pa_s, pb_s) if sweep % 2 == 0 else (pb_s, pa_s)
        factor = chebyshev_factor(sweep, SWEEPS)
        for x in range(1 + sweep, wide - 1 - sweep):
            place = rank_ref[0] * B + (x - WD)
            kept = jnp.where((place >= 0) & (place < rank_ref[3]), 1.0, 0.0)
            middle = old[x]
            around = (old[x + 1] + old[x - 1]) + ysum(middle) + zsum(middle)
            value = middle + factor * (src_s[x] + around * inv_s[x] - middle)
            new[x] = jnp.where(inside, value, 0.0) * kept
    last = pb_s if SWEEPS % 2 == 1 else pa_s
    rows = slice(WD, WD + B)
    for x in range(B):
        plane = last[WD + x]
        slopes = (last[WD + x + 1] - last[WD + x - 1], ydiff(plane), zdiff(plane))
        newp_ref[x * B : x * B + B, :] = plane[rows, 0:S]
        for k in range(3):
            slope = 0.5 * slopes[k]
            at = (k * B + x) * B
            grad_s[at : at + B, :] = slope[rows, 0:S]
            newv_ref[at : at + B, :] = (mid_s[k, WD + x] - GAS_STEP * slope)[rows, 0:S]

    joined = (
        newv_ref[0:S, :],
        jnp.concatenate([newv_ref[S : S + 64, :], grad_s[0:64, :]], axis=0),
        grad_s[64:192, :],
    )
    for v in range(3):
        field_s[:, v * S : v * S + S] = joined[v].T
    pair_s[...] = jnp.zeros((4, S, 2 * S), jnp.float32)

    def some_cells(step, carry):
        for i in range(4):
            cell = step * 4 + i

            def row_of(f):
                return state_ref[pl.ds(f * L2 + 1 + cell, 1), :]

            plane_w = plane_weights(row_of(0), row_of(1))
            wz = axis_weights(row_of(2))
            pair_s[i, 0:64, 0:S] = plane_w
            pair_s[i, 64:S, S : 2 * S] = plane_w
            start = pl.multiple_of(cell * 8, 8)
            left = jnp.concatenate(
                [field_s[pl.ds(start, 8), v * S : v * S + S] for v in range(3)], axis=0
            )
            part = jnp.dot(
                left, pair_s[i], precision=HIGHEST, preferred_element_type=jnp.float32
            )
            for v in range(3):
                for odd in range(2):
                    value = part[v * 8 : v * 8 + 8, odd * S : odd * S + S] * wz
                    sum_s[pl.ds((2 * v + odd) * 16 + cell, 1), :] = jnp.sum(
                        value, axis=0, keepdims=True
                    )
        return carry

    lax.fori_loop(0, PZ // 4, some_cells, 0)
    for f in range(3):
        speed = state_ref[(3 + f) * L2 + 1 : (3 + f) * L2 + 17, :]
        gas = sum_s[f * 16 : f * 16 + 16, :]
        slope = sum_s[(3 + f) * 16 : (3 + f) * 16 + 16, :]
        sent_ref[:, f * S : f * S + S] = state_ref[f * L2 + 1 : f * L2 + 17, :]
        sent_ref[:, (3 + f) * S : (3 + f) * S + S] = (
            speed + COUPLE_STEP * (PARTICLE_DRAG * gas - slope)
        ) / (1.0 + COUPLE_STEP * PARTICLE_DRAG)


def gas_and_sample(ranks, gas, deposits, state):
    wide = B + 2 * WD
    ring = 2 * S
    vmem = pl.BlockSpec(memory_space=pltpu.VMEM)
    return pl.pallas_call(
        gas_kernel,
        out_shape=[
            jax.ShapeDtypeStruct((PZ, 6 * S), jnp.float32),
            jax.ShapeDtypeStruct((3 * 64, S), jnp.float32),
            jax.ShapeDtypeStruct((64, S), jnp.float32),
        ],
        in_specs=[pl.BlockSpec(memory_space=pltpu.SMEM)] + [vmem] * 11,
        scratch_shapes=[
            pltpu.VMEM((4, B + 2 * WG, 24, ring), jnp.float32),
            pltpu.VMEM((B + 2 * WG, 24, S), jnp.float32),
            pltpu.VMEM((4, wide, wide, ring), jnp.float32),
            pltpu.VMEM((wide, wide, S), jnp.float32),
            pltpu.VMEM((3, wide, wide, ring), jnp.float32),
            pltpu.VMEM((3, wide, wide, ring), jnp.float32),
            pltpu.VMEM((wide, wide, ring), jnp.float32),
            pltpu.VMEM((wide, wide, ring), jnp.float32),
            pltpu.VMEM((wide, wide, ring), jnp.float32),
            pltpu.VMEM((wide, wide, ring), jnp.float32),
            pltpu.VMEM((3 * 64, S), jnp.float32),
            pltpu.VMEM((S, 3 * S), jnp.float32),
            pltpu.VMEM((4, S, 2 * S), jnp.float32),
            pltpu.VMEM((96, S), jnp.float32),
        ],
        name="gas_sample",
    )(ranks, *gas, *deposits, state)


def body(position, velocity, radius, cell_count, gas_velocity, pressure):
    axes = ("gx", "gy", "gz")
    rank = lax.axis_index("gz")
    count = lax.axis_size("gz")
    ranks = jnp.stack(
        [lax.axis_index(a) for a in axes]
        + [jnp.int32(lax.axis_size(a) * n) for a, n in zip(axes, (B, B, S))]
    )
    live = jnp.arange(S, dtype=jnp.int32) < cell_count[0, 0][:, None]
    kept = jnp.where(live, radius[0, 0], 0.0)
    state = jnp.concatenate([position[:, 0, 0], velocity[:, 0, 0], kept[None]], axis=0)
    rows = jnp.swapaxes(state, 0, 1).reshape(PZ, 7 * S)
    blank = jnp.zeros_like(rows[:1])
    below = jnp.concatenate([blank, rows[:-1]], axis=0)
    above = jnp.concatenate([rows[1:], blank], axis=0)
    extra = jnp.where(rank >= count - 3, below, jnp.where(rank < 3, above, 0.0))
    gas = jnp.concatenate([gas_velocity, pressure[None]], axis=0)
    edge_size = 4 * B * B * WG
    low_edge = gas[..., :WG].reshape(1, edge_size)
    high_edge = gas[..., S - WG :].reshape(1, edge_size)
    target = jnp.arange(PZ, dtype=jnp.int32)[:, None]
    edges = jnp.where(
        target == rank + 1, high_edge, jnp.where(target == rank - 1, low_edge, 0.0)
    )
    sent = jnp.concatenate([rows, extra, edges], axis=1)
    got = lax.all_to_all(sent, "gz", split_axis=0, concat_axis=0, tiled=True)
    layers = jnp.concatenate(
        [got[PZ - 3 :, 7 * S : 14 * S], got[:, : 7 * S], got[:3, 7 * S : 14 * S]], axis=0
    )
    own = jnp.swapaxes(layers.reshape(L0, 7, S), 0, 1).reshape(7 * L0, S)
    from_low = lax.dynamic_index_in_dim(got, jnp.maximum(rank - 1, 0), 0, keepdims=False)
    from_high = lax.dynamic_index_in_dim(got, jnp.minimum(rank + 1, count - 1), 0, keepdims=False)
    zlo = jnp.where(rank > 0, from_low[14 * S :], 0.0).reshape(4, B * B, WG)
    zhi = jnp.where(rank < count - 1, from_high[14 * S :], 0.0).reshape(4, B * B, WG)
    packed = jnp.concatenate([zhi, jnp.zeros((4, B * B, 32 - 2 * WG), jnp.float32), zlo], axis=2)
    packed = jnp.swapaxes(packed, 0, 1).reshape(B * B, S)
    gas5 = jnp.concatenate([gas.reshape(4 * B * B, S), packed], axis=0)

    def y_slab(first):
        return gas5.reshape(5, B, B, S)[:, :, first : first + WG].reshape(5 * B * WG, S)

    def x_slab(ylo, yhi, first, at, width, block):
        parts = [block.reshape(5, B, B * S)[:, first : first + width].reshape(-1, S)]
        for part in (ylo, yhi):
            part = part[at:].reshape(5, B, width * S)[:, first : first + width]
            parts.append(part.reshape(-1, S))
        return parts

    ylo, yhi = shift_pair(own, own, "gy")
    column = jnp.concatenate([ylo, own, yhi], axis=0)
    xlo, xhi = shift_pair(column, column, "gx")
    first = (own, ylo, yhi, xlo, xhi)
    (moved,) = contact(L1, False, first, first)

    ylo, yhi = shift_pair(
        jnp.concatenate([moved, y_slab(0)], axis=0),
        jnp.concatenate([moved, y_slab(B - WG)], axis=0),
        "gy",
    )
    column = [ylo[: 6 * L1], moved, yhi[: 6 * L1]]
    xlo, xhi = shift_pair(
        jnp.concatenate(column + x_slab(ylo, yhi, 0, 6 * L1, WG, gas5), axis=0),
        jnp.concatenate(column + x_slab(ylo, yhi, B - WG, 6 * L1, WG, gas5), axis=0),
        "gx",
    )
    final, dep, dep_low, dep_high = contact(L2, True, (moved, ylo, yhi, xlo, xhi), first)

    dylo, dyhi = shift_pair(dep_low, dep_high, "gy")
    dxlo, dxhi = shift_pair(
        jnp.concatenate(x_slab(dylo, dyhi, 0, 0, WD, dep), axis=0),
        jnp.concatenate(x_slab(dylo, dyhi, B - WD, 0, WD, dep), axis=0),
        "gx",
    )
    sent_back, new_velocity, new_pressure = gas_and_sample(
        ranks, (gas5, ylo, yhi, xlo, xhi), (dep, dylo, dyhi, dxlo, dxhi), final
    )
    returned = lax.all_to_all(sent_back, "gz", split_axis=0, concat_axis=0, tiled=True)
    returned = jnp.swapaxes(returned.reshape(PZ, 6, S), 0, 1)[:, None, None]
    return (
        returned[:3],
        returned[3:],
        new_velocity.reshape(3, B, B, S),
        new_pressure.reshape(B, B, S),
    )


def solution(mesh):
    placed = (
        P(None, "gx", "gy", "gz", None),
        P(None, "gx", "gy", "gz", None),
        P("gx", "gy", "gz", None),
        P("gx", "gy", "gz"),
        P(None, "gx", "gy", "gz"),
        P("gx", "gy", "gz"),
    )
    return jax.shard_map(
        body,
        mesh=mesh,
        in_specs=placed,
        out_specs=(
            P(None, "gx", "gy", "gz", None),
            P(None, "gx", "gy", "gz", None),
            P(None, "gx", "gy", "gz"),
            P("gx", "gy", "gz"),
        ),
        check_vma=False,
    )
```

time: 199 us -> 157 us (0.79); the launches traced: 199 us -> 154 us
  starting transfers between devices: 84.3 us -> 42.6 us
  other arithmetic: 17.4 us -> 2.88 us
  blocking collectives: 0 us -> 13.2 us
  Pallas kernels: 52.3 us -> 42.8 us
  waiting for transfers between devices: 31.9 us -> 37.4 us
  local copies, waits for them, and re-layouts: 11.3 us -> 13.9 us
    ppermute x11 -> x6, starting transfers between devices: 53.8 us -> 27.3 us  [shift_pair(): from_below = lax.ppermute(array_high, axis, forward)]
    all_to_all x0 -> x1, blocking collectives: none -> 13.2 us  [body(): lax.all_to_all(sent_back, 'gz', split_axis=0, concat_axis=0, tiled=True)]
    pallas_call x3, Pallas kernels: 52.3 us -> 42.8 us  [the longest x2 37.2 us: contact(): pl.pallas_call(lambda *refs: contact_kernel(cells, deposit, *refs), out_s...]
    ppermute x11 -> x6, starting transfers between devices: 16.2 us -> 7.92 us  [shift_pair(): from_above = lax.ppermute(array_low, axis, backward)]
    all_to_all x2 -> x0, starting transfers between devices: 6.95 us -> none  [back(): lax.all_to_all(sent_back, 'gz', split_axis=0, concat_axis=0, tiled=True)]
    all_to_all x1, waiting for transfers between devices: 0.01 us -> 6.56 us  [body(): got = lax.all_to_all(sent, 'gz', split_axis=0, concat_axis=0, tiled=True)]
    unnamed x74 -> x45, local copies, waits for them, and re-layouts: 2.77 us -> 8.15 us
    concatenate x10, other arithmetic: 5.65 us -> 1.14 us  [the longest x1 0.85 us: body(): jnp.concatenate([moved, y_slab(0)], axis=0)]
  transfers between devices with their start and end apart: 25 -> 13, of which waited for: 9 -> 9; matrix products, arithmetic and copies ran while one was open for 10% -> 2% of each run, Pallas kernels for 14% -> 0%
where the time goes in v1:
time: 157 us; the launch traced here: 154 us
  Pallas kernels  42.8 us (27%)
  starting transfers between devices  42.6 us (27%)
  waiting for transfers between devices  37.4 us (24%)
  local copies, waits for them, and re-layouts  13.9 us (9%)
  blocking collectives  13.2 us (8%)
  other arithmetic  2.88 us (2%)
    pallas_call x2, Pallas kernels, contact(): pl.pallas_call(lambda *refs: contact_kernel(cells, deposit, *refs), out_s...  37.2 us
    ppermute x6, waiting for transfers between devices, shift_pair(): from_above = lax.ppermute(array_low, axis, backward)  28.7 us
    ppermute x6, starting transfers between devices, shift_pair(): from_below = lax.ppermute(array_high, axis, forward)  27.3 us
    all_to_all x1, blocking collectives, body(): lax.all_to_all(sent_back, 'gz', split_axis=0, concat_axis=0, tiled=True)  13.2 us
    unnamed x45, local copies, waits for them, and re-layouts  8.15 us
    ppermute x6, starting transfers between devices, shift_pair(): from_above = lax.ppermute(array_low, axis, backward)  7.92 us
    all_to_all x1, starting transfers between devices, body(): got = lax.all_to_all(sent, 'gz', split_axis=0, concat_axis=0, tiled=True)  7.33 us
    all_to_all x1, waiting for transfers between devices, body(): got = lax.all_to_all(sent, 'gz', split_axis=0, concat_axis=0, tiled=True)  6.56 us
  transfers between devices with their start and end apart: 13, of which 9 were waited for; matrix products, arithmetic and copies ran while one was open for 2% of the time, Pallas kernels for 0%

profile of v1, /device:TPU:1, one launch (start us, length us, event | category | flops | bytes accessed | tf_op | source)
XLA Modules:
  0.0 154.1 jit_solution(15414986993690510589)
XLA Ops:
  3.0 0.8 copy-done.11
  4.5 0.8 all_to_all.14
  5.3 7.3 %all-to-all-start = ((f32[16,1,3072]{2,1,0:T(1,128)}), f32[16,1,3072]{2,1,0:T(1,128)S(1)}, u32[]{:S(2)}, u32[]{:S(2)}) async-start(f32[16,1,3072]{2,1,0:T(1,128)} %all_to_all.14), calls=%async_computation | async-start | bytes 393216 | tf_op jit(solution)/shard_map/all_to_all | solution.py:555
  12.7 6.6 %all-to-all-done = f32[16,1,3072]{2,1,0:T(1,128)S(1)} async-done(((f32[16,1,3072]{2,1,0:T(1,128)}), f32[16,1,3072]{2,1,0:T(1,128)S(1)}, u32[]{:S(2)}, u32[]{:S(2)}) %all-to-all-start) | async-done | bytes 196640 | tf_op jit(solution)/shard_map/all_to_all | solution.py:555
  19.4 1.3 collective-permute-start.1
  20.7 5.5 %collective-permute-start = (f32[154,128]{1,0:T(8,128)S(1)}, f32[154,128]{1,0:T(8,128)S(1)}, u32[]{:S(2)}, u32[]{:S(2)}) collective-permute-start(f32[154,128]{1,0:T(8,128)S(1)} %reshape.192.refs_0_.refs_5_), channel_id=1, source_target_pairs={{0,16},{16,32},{32,48},{1,17},{17,33},{33,49},{2,18},{18,34},{34,5... | collective-permute-start | bytes 236552 | tf_op jit(solution)/shard_map/ppermute | solution.py:42
  27.2 1.4 collective-permute-done.1.refs_2_.refs_7_
  29.3 1.3 collective-permute-start.3
  30.6 4.0 %collective-permute-start.2 = (f32[462,128]{1,0:T(8,128)S(1)}, f32[462,128]{1,0:T(8,128)S(1)}, u32[]{:S(2)}, u32[]{:S(2)}) collective-permute-start(f32[462,128]{1,0:T(8,128)S(1)} %pad_maximum_fusion), channel_id=1, source_target_pairs={{0,64},{64,128},{128,192},{1,65},{65,129},{129,193},{2,66},{66,130... | collective-permute-start | bytes 709640 | tf_op jit(solution)/shard_map/ppermute | solution.py:42
  34.7 3.0 %collective-permute-done.3.refs_4_.refs_9_ = f32[462,128]{1,0:T(8,128)S(1)} collective-permute-done((f32[462,128]{1,0:T(8,128)S(1)}, f32[462,128]{1,0:T(8,128)S(1)}, u32[]{:S(2)}, u32[]{:S(2)}) %collective-permute-start.3) | collective-permute-done | bytes 236576 | tf_op jit(solution)/shard_map/ppermute | solution.py:43
  37.6 0.9 collective-permute-done.2.refs_3_.refs_8_
  39.2 18.1 %contact.1.refs_0_ = f32[120,128]{1,0:T(8,128)} custom-call(f32[154,128]{1,0:T(8,128)} %copy-done.3, f32[154,128]{1,0:T(8,128)} %copy-done.10, f32[154,128]{1,0:T(8,128)} %copy-done.9, f32[462,128]{1,0:T(8,128)} %copy-done.2, f32[462,128]{1,0:T(8,128)} %copy-done.1, f32[154,128]{1,0:T(8,128)} %copy-done.3, f32[154,128]{1,0:T(8,128)} %copy-done.10, ...), custom_call_target="tpu_custom_call" | custom-call | tf_op jit(solution)/shard_map/contact/pallas_call | solution.py:313
  57.4 0.8 pad_maximum_fusion.2
  58.2 1.3 collective-permute-start.5
  59.6 6.4 %collective-permute-start.4 = (f32[320,128]{1,0:T(8,128)S(1)}, f32[320,128]{1,0:T(8,128)S(1)}, u32[]{:S(2)}, u32[]{:S(2)}) collective-permute-start(f32[320,128]{1,0:T(8,128)S(1)} %get-tuple-element.49), channel_id=1, source_target_pairs={{0,16},{16,32},{32,48},{1,17},{17,33},{33,49},{2,18},{18,34},{34,5... | collective-permute-start | bytes 491528 | tf_op jit(solution)/shard_map/ppermute | solution.py:42
  66.0 5.8 %collective-permute-done.5.refs_2_.refs_3_ = f32[320,128]{1,0:T(8,128)S(1)} collective-permute-done((f32[320,128]{1,0:T(8,128)S(1)}, f32[320,128]{1,0:T(8,128)S(1)}, u32[]{:S(2)}, u32[]{:S(2)}) %collective-permute-start.5) | collective-permute-done | bytes 163872 | tf_op jit(solution)/shard_map/ppermute | solution.py:43
  72.7 0.8 copy-done.6
  73.8 1.3 collective-permute-start.7
  75.4 5.2 %collective-permute-start.6 = (f32[810,128]{1,0:T(8,128)S(1)}, f32[810,128]{1,0:T(8,128)S(1)}, u32[]{:S(2)}, u32[]{:S(2)}) collective-permute-start(f32[810,128]{1,0:T(8,128)S(1)} %concatenate.56), channel_id=1, source_target_pairs={{0,64},{64,128},{128,192},{1,65},{65,129},{129,193},{2,66},{66,130... | collective-permute-start | bytes 1244168 | tf_op jit(solution)/shard_map/ppermute | solution.py:42
  80.6 7.2 %collective-permute-done.7.refs_4_.refs_5_ = f32[810,128]{1,0:T(8,128)S(1)} collective-permute-done((f32[810,128]{1,0:T(8,128)S(1)}, f32[810,128]{1,0:T(8,128)S(1)}, u32[]{:S(2)}, u32[]{:S(2)}) %collective-permute-start.7) | collective-permute-done | bytes 414752 | tf_op jit(solution)/shard_map/ppermute | solution.py:43
  87.9 1.2 collective-permute-done.6.refs_3_.refs_4_
  89.8 19.0 %contact_deposit.1 = (f32[108,128]{1,0:T(8,128)}, f32[320,128]{1,0:T(8,128)}, f32[160,128]{1,0:T(8,128)}, f32[160,128]{1,0:T(8,128)}) custom-call(f32[120,128]{1,0:T(8,128)} %contact.1.refs_0_, f32[320,128]{1,0:T(8,128)} %copy-done.8, f32[320,128]{1,0:T(8,128)} %copy-done.7, f32[810,128]{1,0:T(8,128)} %copy-done.5, f32[810,128]{1,0:T(8,128)} %copy-done.4, ...), custom_call_target="tpu_custom_call" | custom-call | tf_op jit(solution)/shard_map/contact_deposit/pallas_call | solution.py:313
  108.8 1.3 collective-permute-start.8
  110.1 1.3 collective-permute-start.9
  111.4 0.9 reshape.205
  113.2 7.4 %collective-permute-done.9.refs_8_ = f32[160,128]{1,0:T(8,128)S(1)} collective-permute-done((f32[160,128]{1,0:T(8,128)}, f32[160,128]{1,0:T(8,128)S(1)}, u32[]{:S(2)}, u32[]{:S(2)}) %collective-permute-start.9) | collective-permute-done | bytes 81952 | tf_op jit(solution)/shard_map/ppermute | solution.py:43
  121.3 4.9 %collective-permute-start.10 = (f32[320,128]{1,0:T(8,128)S(1)}, f32[320,128]{1,0:T(8,128)S(1)}, u32[]{:S(2)}, u32[]{:S(2)}) collective-permute-start(f32[320,128]{1,0:T(8,128)S(1)} %pad_maximum_fusion.6), channel_id=1, source_target_pairs={{0,64},{64,128},{128,192},{1,65},{65,129},{129,193},{2,66},{66,130... | collective-permute-start | bytes 491528 | tf_op jit(solution)/shard_map/ppermute | solution.py:42
  126.3 1.5 collective-permute-start.11
  128.5 3.8 %collective-permute-done.11.refs_10_ = f32[320,128]{1,0:T(8,128)S(1)} collective-permute-done((f32[320,128]{1,0:T(8,128)S(1)}, f32[320,128]{1,0:T(8,128)S(1)}, u32[]{:S(2)}, u32[]{:S(2)}) %collective-permute-start.11) | collective-permute-done | bytes 163872 | tf_op jit(solution)/shard_map/ppermute | solution.py:43
  133.0 5.7 %gas_sample.1 = (f32[16,768]{1,0:T(8,128)}, f32[192,128]{1,0:T(8,128)}, f32[64,128]{1,0:T(8,128)}) custom-call(s32[6]{0:T(128)} %stack.15.refs_0_, f32[320,128]{1,0:T(8,128)} %copy-done, f32[320,128]{1,0:T(8,128)} %copy-done.8, f32[320,128]{1,0:T(8,128)} %copy-done.7, f32[810,128]{1,0:T(8,128)} %copy-done.5, f32[810,128]{1,0:T(8,128)} %copy-done.4, ...), custom_call_target="tpu_custom_call" | custom-call | tf_op jit(solution)/shard_map/gas_sample/pallas_call | solution.py:502
  138.7 0.8 copy.27
  139.5 13.2 %all_to_all.21 = f32[16,1,768]{2,1,0:T(1,128)S(1)} all-to-all(f32[16,1,768]{2,1,0:T(1,128)S(1)} %copy.27), channel_id=1, replica_groups=mesh['gx'=4,'gy'=4,'gz'=16] {'gz'}, dimensions={0} | all-to-all | bytes 98304 | tf_op jit(solution)/shard_map/all_to_all | solution.py:606
  (119 shorter events, 11.7 us)
Async XLA Ops:
  0.6 0.7 copy-start.18
  0.6 1.4 copy-start.17
  2.9 0.9 copy-start.11
  3.0 0.9 copy-start.16
  5.3 14.0 %all-to-all-start = ((f32[16,1,3072]{2,1,0:T(1,128)}), f32[16,1,3072]{2,1,0:T(1,128)S(1)}, u32[]{:S(2)}, u32[]{:S(2)}) async-start(f32[16,1,3072]{2,1,0:T(1,128)} %all_to_all.14), calls=%async_computation | async-start | bytes 393216 | tf_op jit(solution)/shard_map/all_to_all | solution.py:555
  19.4 9.2 %copy-start.3 = (f32[154,128]{1,0:T(8,128)}, f32[154,128]{1,0:T(8,128)S(1)}, u32[]{:S(2)}) copy-start(f32[154,128]{1,0:T(8,128)S(1)} %reshape.192.refs_0_.refs_5_) | copy-start | bytes 236548
  19.4 9.2 %collective-permute-start.1 = (f32[154,128]{1,0:T(8,128)S(1)}, f32[154,128]{1,0:T(8,128)S(1)}, u32[]{:S(2)}, u32[]{:S(2)}) collective-permute-start(f32[154,128]{1,0:T(8,128)S(1)} %reshape.192.refs_0_.refs_5_), channel_id=1, source_target_pairs={{16,0},{32,16},{48,32},{17,1},{33,17},{49,33},{18,2},{34,18},{50,3... | collective-permute-start | bytes 236552 | tf_op jit(solution)/shard_map/ppermute | solution.py:43
  20.7 7.9 %collective-permute-start = (f32[154,128]{1,0:T(8,128)S(1)}, f32[154,128]{1,0:T(8,128)S(1)}, u32[]{:S(2)}, u32[]{:S(2)}) collective-permute-start(f32[154,128]{1,0:T(8,128)S(1)} %reshape.192.refs_0_.refs_5_), channel_id=1, source_target_pairs={{0,16},{16,32},{32,48},{1,17},{17,33},{33,49},{2,18},{18,34},{34,5... | collective-permute-start | bytes 236552 | tf_op jit(solution)/shard_map/ppermute | solution.py:42
  27.1 7.4 %copy-start = (f32[320,128]{1,0:T(8,128)}, f32[320,128]{1,0:T(8,128)S(1)}, u32[]{:S(2)}) copy-start(f32[320,128]{1,0:T(8,128)S(1)} %pad_maximum_fusion.5.refs_1_) | copy-start | bytes 491524
  28.6 0.6 copy-start.9
  28.6 0.7 copy-start.10
  29.3 8.4 %collective-permute-start.3 = (f32[462,128]{1,0:T(8,128)S(1)}, f32[462,128]{1,0:T(8,128)S(1)}, u32[]{:S(2)}, u32[]{:S(2)}) collective-permute-start(f32[462,128]{1,0:T(8,128)S(1)} %pad_maximum_fusion), channel_id=1, source_target_pairs={{64,0},{128,64},{192,128},{65,1},{129,65},{193,129},{66,2},{130,66... | collective-permute-start | bytes 709640 | tf_op jit(solution)/shard_map/ppermute | solution.py:43
  30.6 8.0 %collective-permute-start.2 = (f32[462,128]{1,0:T(8,128)S(1)}, f32[462,128]{1,0:T(8,128)S(1)}, u32[]{:S(2)}, u32[]{:S(2)}) collective-permute-start(f32[462,128]{1,0:T(8,128)S(1)} %pad_maximum_fusion), channel_id=1, source_target_pairs={{0,64},{64,128},{128,192},{1,65},{65,129},{129,193},{2,66},{66,130... | collective-permute-start | bytes 709640 | tf_op jit(solution)/shard_map/ppermute | solution.py:42
  37.6 0.9 copy-start.1
  38.5 0.7 copy-start.2
  58.2 13.6 %collective-permute-start.5 = (f32[320,128]{1,0:T(8,128)S(1)}, f32[320,128]{1,0:T(8,128)S(1)}, u32[]{:S(2)}, u32[]{:S(2)}) collective-permute-start(f32[320,128]{1,0:T(8,128)S(1)} %get-tuple-element.48), channel_id=1, source_target_pairs={{16,0},{32,16},{48,32},{17,1},{33,17},{49,33},{18,2},{34,18},{50,3... | collective-permute-start | bytes 491528 | tf_op jit(solution)/shard_map/ppermute | solution.py:43
  59.6 12.3 %collective-permute-start.4 = (f32[320,128]{1,0:T(8,128)S(1)}, f32[320,128]{1,0:T(8,128)S(1)}, u32[]{:S(2)}, u32[]{:S(2)}) collective-permute-start(f32[320,128]{1,0:T(8,128)S(1)} %get-tuple-element.49), channel_id=1, source_target_pairs={{0,16},{16,32},{32,48},{1,17},{17,33},{33,49},{2,18},{18,34},{34,5... | collective-permute-start | bytes 491528 | tf_op jit(solution)/shard_map/ppermute | solution.py:42
  71.9 0.7 copy-start.7
  72.0 0.7 copy-start.8
  72.7 0.8 copy-start.6
  73.8 14.1 %collective-permute-start.7 = (f32[810,128]{1,0:T(8,128)S(1)}, f32[810,128]{1,0:T(8,128)S(1)}, u32[]{:S(2)}, u32[]{:S(2)}) collective-permute-start(f32[810,128]{1,0:T(8,128)S(1)} %concatenate.57), channel_id=1, source_target_pairs={{64,0},{128,64},{192,128},{65,1},{129,65},{193,129},{66,2},{130,66... | collective-permute-start | bytes 1244168 | tf_op jit(solution)/shard_map/ppermute | solution.py:43
  75.4 13.7 %collective-permute-start.6 = (f32[810,128]{1,0:T(8,128)S(1)}, f32[810,128]{1,0:T(8,128)S(1)}, u32[]{:S(2)}, u32[]{:S(2)}) collective-permute-start(f32[810,128]{1,0:T(8,128)S(1)} %concatenate.56), channel_id=1, source_target_pairs={{0,64},{64,128},{128,192},{1,65},{65,129},{129,193},{2,66},{66,130... | collective-permute-start | bytes 1244168 | tf_op jit(solution)/shard_map/ppermute | solution.py:42
  87.9 1.2 copy-start.4
  89.1 0.7 copy-start.5
  108.8 3.7 %collective-permute-start.8 = (f32[160,128]{1,0:T(8,128)}, f32[160,128]{1,0:T(8,128)S(1)}, u32[]{:S(2)}, u32[]{:S(2)}) collective-permute-start(f32[160,128]{1,0:T(8,128)} %get-tuple-element.12), channel_id=1, source_target_pairs={{0,16},{16,32},{32,48},{1,17},{17,33},{33,49},{2,18},{18,34},{34,5... | collective-permute-start | bytes 245768 | tf_op jit(solution)/shard_map/ppermute | solution.py:42
  110.1 10.5 %collective-permute-start.9 = (f32[160,128]{1,0:T(8,128)}, f32[160,128]{1,0:T(8,128)S(1)}, u32[]{:S(2)}, u32[]{:S(2)}) collective-permute-start(f32[160,128]{1,0:T(8,128)} %get-tuple-element.13), channel_id=1, source_target_pairs={{16,0},{32,16},{48,32},{17,1},{33,17},{49,33},{18,2},{34,18},{50,3... | collective-permute-start | bytes 245768 | tf_op jit(solution)/shard_map/ppermute | solution.py:43
  112.5 0.6 copy-start.12
  120.6 0.6 copy-start.13
  121.3 7.2 %collective-permute-start.10 = (f32[320,128]{1,0:T(8,128)S(1)}, f32[320,128]{1,0:T(8,128)S(1)}, u32[]{:S(2)}, u32[]{:S(2)}) collective-permute-start(f32[320,128]{1,0:T(8,128)S(1)} %pad_maximum_fusion.6), channel_id=1, source_target_pairs={{0,64},{64,128},{128,192},{1,65},{65,129},{129,193},{2,66},{66,130... | collective-permute-start | bytes 491528 | tf_op jit(solution)/shard_map/ppermute | solution.py:42
  126.3 6.1 %collective-permute-start.11 = (f32[320,128]{1,0:T(8,128)S(1)}, f32[320,128]{1,0:T(8,128)S(1)}, u32[]{:S(2)}, u32[]{:S(2)}) collective-permute-start(f32[320,128]{1,0:T(8,128)S(1)} %pad_maximum_fusion.7), channel_id=1, source_target_pairs={{64,0},{128,64},{192,128},{65,1},{129,65},{193,129},{66,2},{130,66... | collective-permute-start | bytes 491528 | tf_op jit(solution)/shard_map/ppermute | solution.py:43
  128.5 3.9 %copy-start.14 = (f32[320,128]{1,0:T(8,128)}, f32[320,128]{1,0:T(8,128)S(1)}, u32[]{:S(2)}) copy-start(f32[320,128]{1,0:T(8,128)S(1)} %collective-permute-done.10.refs_9_) | copy-start | bytes 491524
  132.4 0.7 copy-start.15
